TPU v7x, 32 devices: a whole 2x2x4 slice. The times are simulated.
32 devices in a mesh: az: 16 (over z, y, x), rad: 2 (over core).
Axes of the slice: x: 2, y: 2, z: 4, core: 2. Of those that a mesh axis runs over, the one named last changes fastest.
Arguments:
- state: float32 [5, 2, 512, 256], P(None, None, 'az', 'rad'), as said below
- shifts: int32 [256], P('rad'), may hold values from 4 to 96, as said below
Outputs:
- state_out: float32 [5, 2, 512, 256], P(None, None, 'az', 'rad')
Inputs may be any that keep to these rules, and one draw needn't show every extreme that they name: `state`: density lies between 0.3 and 3, each velocity component (momentum over density) between -1 and 1, and energy exceeds the kinetic energy by at least 0.8 times density. `shifts`: both 4 and 96 occur.
All inputs are finite; a program needn't handle non-finite values.
Results may differ from a plain program's by a relative error of at most 0.0003.
Values sent between devices are 32-bit elements; how exact they have to be, the bound alone decides.
A program may use at most 64 MiB of HBM per device.

v0:
```python
import functools

import jax
import jax.numpy as jnp
from jax import lax
from jax.experimental import pallas as pl
from jax.experimental.pallas import tpu as pltpu
from jax.sharding import PartitionSpec as P

STEPS = 2
SMIN = 4
SMAX = 96
EDGE = 4
TILE = 8

GAMMA_GAS = 1.4
COURANT_RADIAL = 0.15
COURANT_AZIMUTH = 0.15
VISCOSITY_COEF = 1.0


def up(x, axis):
    return pltpu.roll(x, x.shape[axis] - 1, axis)


def down(x, axis):
    return pltpu.roll(x, 1, axis)


def face_speeds(velocity, axis, courant):
    face = (0.5 * courant) * (velocity + up(velocity, axis))
    return jnp.maximum(face, 0.0), jnp.minimum(face, 0.0)


def advect(field, speeds, axis):
    low = field - down(field, axis)
    high = up(low, axis)
    product = low * high
    positive = product > 0
    half = jnp.where(positive, product / jnp.where(positive, low + high, 1.0), 0.0)
    flux = speeds[0] * (field + half) + speeds[1] * up(field - half, axis)
    return flux - down(flux, axis)


def push(pressure, density, speed, axis, courant):
    compress = jnp.minimum(up(speed, axis) - down(speed, axis), 0.0)
    total = pressure + VISCOSITY_COEF * density * compress * compress
    work = total * speed
    scale = -0.5 * courant
    return scale * (up(total, axis) - down(total, axis)), scale * (up(work, axis) - down(work, axis))


def shifted(window, shift_left, rows, longest):
    bits = longest.bit_length()
    x = window
    for bit in reversed(range(bits)):
        stride = 1 << bit
        left = stride - 1
        if stride >= TILE:
            keep = -(-(rows + left) // TILE) * TILE
            chosen = min(keep, x.shape[0] - stride)
            mask = (jnp.broadcast_to(shift_left, (chosen, shift_left.shape[1])) & stride) != 0
            y = jnp.where(mask, x[stride : stride + chosen], x[:chosen])
            x = y if chosen == keep else jnp.concatenate([y, x[chosen:keep]], axis=0)
        else:
            mask = (jnp.broadcast_to(shift_left, x.shape) & stride) != 0
            x = jnp.where(mask, pltpu.roll(x, x.shape[0] - stride, 0), x)
    return x[:rows]


def kernel(n_az, n_rad, x_in, shifts, out, *scratch):
    (x, load_sem, A, W0, W1, O0, O1, L0, R0, L1, R1, L2, R2, state_send, state_recv, gather_send, gather_recv,
     side_send, side_recv) = scratch
    fields, depth, width, lanes = x.shape
    behind = SMAX + EDGE
    whole = behind // width
    tail = behind % width
    tail_rows = -(-tail // TILE) * TILE
    group = whole + 1
    base = group * width
    first_row = width - tail_rows
    me = lax.axis_index("az")
    place = lax.rem(me, group)
    position = lax.axis_index("rad")

    def az(by):
        return {"az": lax.rem(me + by + n_az, n_az)}

    def member(by):
        return {"az": me - place + lax.rem(place + by + group, group)}

    def rad(by):
        return {"rad": position + by}

    barrier = pltpu.get_barrier_semaphore()
    MESH = pl.DeviceIdType.MESH
    load = pltpu.make_async_copy(x_in, x, load_sem)
    load.start()
    for by in (1, -1, -group):
        pl.semaphore_signal(barrier, inc=1, device_id=az(by), device_id_type=MESH)
    for h in range(1, group):
        pl.semaphore_signal(barrier, inc=1, device_id=member(h), device_id_type=MESH)

    has_left = position > 0
    has_right = position < n_rad - 1

    @pl.when(has_left)
    def _():
        pl.semaphore_signal(barrier, inc=1, device_id=rad(-1), device_id_type=MESH)

    @pl.when(has_right)
    def _():
        pl.semaphore_signal(barrier, inc=1, device_id=rad(1), device_id_type=MESH)

    load.wait()
    A[:, :, TILE : TILE + width, :] = x[...]
    beside_me = (position + n_rad - 1) // n_rad + (2 * n_rad - 2 - position) // n_rad
    pl.semaphore_wait(barrier, group + 2 + beside_me)

    def remote(src, dst, send, recv, where):
        return pltpu.make_async_remote_copy(
            src_ref=src, dst_ref=dst, send_sem=send, recv_sem=recv, device_id=where, device_id_type=MESH
        )

    def ring_copies(z):
        return [
            remote(x.at[:, z, width - TILE : width], A.at[:, z, 0:TILE],
                   state_send.at[0, z], state_recv.at[0, z], az(1)),
            remote(x.at[:, z, 0:TILE], A.at[:, z, TILE + width : 2 * TILE + width],
                   state_send.at[1, z], state_recv.at[1, z], az(-1)),
        ]

    def side_copies(phase, src, left_dst, right_dst, z):
        to_right = remote(src.at[:, z], left_dst.at[:, z], side_send.at[phase, 0, z],
                          side_recv.at[phase, 0, z], rad(1))
        to_left = remote(src.at[:, z], right_dst.at[:, z], side_send.at[phase, 1, z],
                         side_recv.at[phase, 1, z], rad(-1))
        return to_right, to_left

    def start_side(*args):
        to_right, to_left = side_copies(*args)

        @pl.when(has_right)
        def _():
            to_right.start()

        @pl.when(has_left)
        def _():
            to_left.start()

    def await_side(*args):
        to_right, to_left = side_copies(*args)

        @pl.when(has_left)
        def _():
            to_right.wait_recv()

        @pl.when(has_right)
        def _():
            to_left.wait_recv()

    def end_side(*args):
        to_right, to_left = side_copies(*args)

        @pl.when(has_right)
        def _():
            to_right.wait_send()

        @pl.when(has_left)
        def _():
            to_left.wait_send()

    windows = (W0, W1)
    rotated = (O0, O1)
    sides = ((x, L0, R0), (O0, L1, R1), (O1, L2, R2))

    def gather_copies(step, f, z):
        W = windows[step]
        own, back = W.at[f, z, base : base + width], W.at[f, z, 0:width]
        sems = lambda h: (gather_send.at[step, h, f, z], gather_recv.at[step, h, f, z])
        onward = remote(own, back, *sems(0), az(group))
        inside = []
        for h in range(1, group):
            dst = W.at[f, z, base - h * width : base - (h - 1) * width]
            inside.append([remote(src, dst, *sems(h), member(h)) for src in (own, back)])
        return onward, inside

    def send_own(step, f, z):
        onward, inside = gather_copies(step, f, z)
        onward.start()
        for h in range(1, group):

            @pl.when(place + h < group)
            def _():
                inside[h - 1][0].start()

    def pass_on(step, f, z):
        onward, inside = gather_copies(step, f, z)
        onward.wait_recv()
        for h in range(1, group):

            @pl.when(place + h >= group)
            def _():
                inside[h - 1][1].start()

    def edges(own, left, right):
        rows = own.shape[0]
        lane = lax.broadcasted_iota(jnp.int32, (rows, lanes), 1)
        at = jnp.full((rows, lanes), position, jnp.int32)
        left = jnp.where(at == 0, jnp.broadcast_to(own[:, 0:1], own.shape), left)
        right = jnp.where(at == n_rad - 1, jnp.broadcast_to(own[:, lanes - 1 : lanes], own.shape), right)
        return jnp.where(lane < lanes // 2, right, left)

    def wide(own, beside):
        return jnp.concatenate([own, beside], axis=1)

    def hydro(step, z, strip, beside):
        rows = slice(TILE, TILE + width)
        tall = [strip(f) for f in range(fields)]
        az_speeds = face_speeds(tall[2] / tall[0], 0, COURANT_AZIMUTH)
        broad = [wide(tall[f][rows], beside(f, tall[f][rows])) for f in range(fields)]
        rad_speeds = face_speeds(broad[1] / broad[0], 1, COURANT_RADIAL)
        for f in range(fields):
            along = advect(tall[f], az_speeds, 0)[rows]
            across = advect(broad[f], rad_speeds, 1)[:, :lanes]
            windows[step][f, z, base : base + width, :] = tall[f][rows] - along - across
            send_own(step, f, z)

    def viscous(z, state, extended):
        rho, mr, mp, mz, energy = state
        own = slice(None) if extended else slice(0, lanes)
        inverse = 1.0 / rho
        pressure = (GAMMA_GAS - 1.0) * (energy - 0.5 * (mr * mr + mp * mp + mz * mz) * inverse)
        az_m, az_e = push(pressure[:, own], rho[:, own], (mp * inverse)[:, own], 0, COURANT_AZIMUTH)
        rad_m, rad_e = push(pressure, rho, mr * inverse, 1, COURANT_RADIAL)
        return [
            rho[:, own],
            mr[:, own] + rad_m[:, own],
            mp[:, own] + az_m,
            mz[:, own],
            energy[:, own] + az_e + rad_e[:, own],
        ]

    count = width + 2 * EDGE

    for z in range(depth):
        for copy in ring_copies(z):
            copy.start()
    for z in range(depth):
        start_side(0, *sides[0], z)
    for z in range(depth):
        for copy in ring_copies(z):
            copy.wait_recv()
        await_side(0, *sides[0], z)
        hydro(0, z, lambda f: A[f, z], lambda f, own: edges(own, L0[f, z], R0[f, z]))

    for step in range(STEPS):
        for z in range(depth):
            for f in range(fields):
                pass_on(step, f, z)
        O, L, R = sides[step + 1]
        for z in range(depth):
            for f in range(fields):
                for copies in gather_copies(step, f, z)[1]:
                    copies[0].wait_recv()
                start = base - first_row - EDGE
                O[f, z] = shifted(windows[step][f, z, first_row:], start - shifts[...], count, start - SMIN)
            start_side(step + 1, O, L, R, z)
        for z in range(depth):
            await_side(step + 1, O, L, R, z)
            state = [wide(O[f, z], edges(O[f, z], L[f, z], R[f, z])) for f in range(fields)]
            if step == STEPS - 1:
                new = viscous(z, state, False)
                for f in range(fields):
                    out[f, z] = new[f][EDGE : EDGE + width]
            else:
                new = viscous(z, state, True)
                A_rows = slice(TILE - EDGE, TILE - EDGE + count)
                for f in range(fields):
                    A[f, z, A_rows, :] = new[f][:, :lanes]
                hydro(
                    step + 1,
                    z,
                    lambda f: A[f, z],
                    lambda f, own: edges(own, *[new[f][EDGE : EDGE + width, lanes:]] * 2),
                )

    for z in range(depth):
        for copy in ring_copies(z):
            copy.wait_send()
        for phase in range(STEPS + 1):
            end_side(phase, *sides[phase], z)
        for step in range(STEPS):
            for f in range(fields):
                onward, inside = gather_copies(step, f, z)
                onward.wait_send()
                for copies in inside:
                    copies[0].wait_send()


def body(mesh, state, shifts):
    n_az, n_rad = mesh.shape["az"], mesh.shape["rad"]
    fields, depth, width, lanes = state.shape
    behind = SMAX + EDGE
    group = behind // width + 1
    window = (group + 1) * width
    count = width + 2 * EDGE
    vmem = lambda rows: pltpu.VMEM((fields, depth, rows, lanes), jnp.float32)
    dma = pltpu.SemaphoreType.DMA
    return pl.pallas_call(
        functools.partial(kernel, n_az, n_rad),
        out_shape=pltpu.VMEM(state.shape, state.dtype),
        in_specs=[pl.BlockSpec(memory_space=pl.ANY), pl.BlockSpec(memory_space=pltpu.VMEM)],
        out_specs=pl.BlockSpec(memory_space=pltpu.VMEM),
        scratch_shapes=[
            vmem(width),
            dma(()),
            vmem(width + 2 * TILE),
            vmem(window),
            vmem(window),
            vmem(count),
            vmem(count),
            vmem(width),
            vmem(width),
            vmem(count),
            vmem(count),
            vmem(count),
            vmem(count),
            dma((2, depth)),
            dma((2, depth)),
            dma((STEPS, group, fields, depth)),
            dma((STEPS, group, fields, depth)),
            dma((STEPS + 1, 2, depth)),
            dma((STEPS + 1, 2, depth)),
        ],
        compiler_params=pltpu.CompilerParams(collective_id=0, has_side_effects=True),
    )(state, shifts.reshape(1, -1))


def solution(mesh):
    in_specs = (P(None, None, "az", "rad"), P("rad"))
    out_specs = P(None, None, "az", "rad")
    return jax.shard_map(
        functools.partial(body, mesh), mesh=mesh, in_specs=in_specs, out_specs=out_specs, check_vma=False
    )
```

profile of v0, /device:TPU:0, one launch (start us, length us, event | category | flops | bytes accessed | tf_op | source)
XLA Modules:
  0.0 36.0 jit_solution(1343813166938977456)
XLA Ops:
  0.0 35.3 %shard_map.28 = f32[5,2,32,128]{3,2,1,0:T(8,128)S(1)} custom-call(f32[5,2,32,128]{3,2,1,0:T(8,128)} %x_in.1, s32[1,128]{1,0:T(1,128)} %bitcast.1), custom_call_target="tpu_custom_call" | custom-call | tf_op jit(solution)/shard_map/pallas_call | solution.py:310
  35.3 0.7 %copy.4 = f32[5,2,32,128]{3,2,1,0:T(8,128)} copy(f32[5,2,32,128]{3,2,1,0:T(8,128)S(1)} %shard_map.28) | data formatting | bytes 327680
where the time goes:
time: 36.4 us; the launch traced here: 36 us
  Pallas kernels  35.3 us (97%)
  local copies, waits for them, and re-layouts  0.67 us (2%)
    pallas_call x1, Pallas kernels, body(): pl.pallas_call(functools.partial(kernel, n_az, n_rad), out_shape=pltpu.VM...  35.3 us

commit v1 on v0

--- a/solution.py
+++ b/solution.py
@@ -337,9 +337,472 @@
     )(state, shifts.reshape(1, -1))
 
 
+GROUPS = 4
+
+
+def lane_rows(x, shift):
+    return pltpu.roll(x, shift % x.shape[1], 1)
+
+
+def regroup(parts, lane):
+    size = parts[0].shape[1] // GROUPS
+    low = (lane & (2 * size)) == 0
+    even = (lane & size) == 0
+    a = [None] * GROUPS
+    for g in range(2):
+        p, q = parts[g], parts[g + 2]
+        a[g] = jnp.where(low, p, lane_rows(q, 2 * size))
+        a[g + 2] = jnp.where(low, lane_rows(p, 2 * size), q)
+    out = []
+    for g in (0, 2):
+        p, q = a[g], a[g + 1]
+        out.append(jnp.where(even, p, lane_rows(q, size)))
+        out.append(jnp.where(even, lane_rows(p, -size), q))
+    return out
+
+
+def fold(x, lane, row):
+    half = x.shape[1] // 2
+    stay = (lane < half) == (row < TILE // 2)
+    return jnp.where(stay, x, lane_rows(pltpu.roll(x, TILE // 2, 0), half))
+
+
+def advect_all(state):
+    rho, mr, mp = state[0], state[1], state[2]
+    inverse = 1.0 / rho
+    az_speeds = face_speeds(mp * inverse, 1, COURANT_AZIMUTH)
+    rad_speeds = face_speeds(mr * inverse, 0, COURANT_RADIAL)
+
+    def step(field):
+        return field - advect(field, az_speeds, 1) - advect(field, rad_speeds, 0)
+
+    return step
+
+
+def push_all(state):
+    rho, mr, mp, mz, energy = state
+    inverse = 1.0 / rho
+    pressure = (GAMMA_GAS - 1.0) * (energy - 0.5 * (mr * mr + mp * mp + mz * mz) * inverse)
+    az_m, az_e = push(pressure, rho, mp * inverse, 1, COURANT_AZIMUTH)
+    rad_m, rad_e = push(pressure, rho, mr * inverse, 0, COURANT_RADIAL)
+    return mr + rad_m, mp + az_m, energy + az_e + rad_e
+
+
+def turned_kernel(n_az, n_rad, x_in, shifts, out, *scratch):
+    (x, T4, EP, EV, W4, WE, other, SC, PA, PB, PE, RA, RB, RE, load_sem, shift_sem, swap_sem, own_send, own_recv,
+     side_send, side_recv, last_send, last_recv, pass_send, pass_recv, back_send, back_recv) = scratch
+    fields, depth, width, lanes = x.shape
+    blocks = n_az // (depth * n_rad)
+    tiles = lanes // TILE
+    rows = 4 * TILE
+    MESH = pl.DeviceIdType.MESH
+    me = lax.axis_index("az")
+    core = lax.axis_index("rad")
+    half = lax.rem(me, n_rad)
+    layer = lax.rem(me // n_rad, depth)
+    block = me // (n_rad * depth)
+    place = (half * blocks + block) * 2 + core
+    partner = {"rad": 1 - core}
+    here = half == core
+
+    def remote(src, dst, send, recv, where):
+        return pltpu.make_async_remote_copy(
+            src_ref=src, dst_ref=dst, send_sem=send, recv_sem=recv, device_id=where, device_id_type=MESH
+        )
+
+    loads = [pltpu.make_async_copy(x_in.at[:, l], x.at[:, l], load_sem.at[l]) for l in range(depth)]
+    for load in loads:
+        load.start()
+    barrier = pltpu.get_barrier_semaphore()
+    for k in range(1, n_az):
+        pl.semaphore_signal(
+            barrier, inc=1, device_id={"az": lax.rem(me + k, n_az), "rad": half}, device_id_type=MESH
+        )
+    pl.semaphore_signal(barrier, inc=1, device_id=partner, device_id_type=MESH)
+
+    lane = lax.broadcasted_iota(jnp.int32, (TILE, lanes), 1)
+    row = lax.broadcasted_iota(jnp.int32, (TILE, lanes), 0)
+    group = lane // width
+
+    for l in range(depth):
+        loads[l].wait()
+        T4[l, 1 : tiles + 1] = x[0:4, l].reshape(4 * width, lanes).T.reshape(tiles, TILE, lanes)
+    energy = x[4].reshape(depth * width, lanes)
+    turned = jnp.concatenate([energy] * (lanes // (depth * width)), axis=0).T.reshape(tiles, TILE, lanes)
+    for l in range(depth):
+        for m in range(tiles // GROUPS):
+            packed = turned[GROUPS * m] if l == 0 else lane_rows(turned[GROUPS * m], -width * l)
+            for g in range(1, GROUPS):
+                packed = jnp.where(group == g, lane_rows(turned[GROUPS * m + g], width * (g - l)), packed)
+            EP[l, 1 + m] = packed
+
+    def pad(l, to, tile_from, energy_from):
+        T4[l, to[0]] = T4[l, tile_from]
+        EP[l, to[1]] = EP[l, energy_from]
+
+    @pl.when(core == 0)
+    def _():
+        for l in range(depth):
+            pad(l, (0, 0), 1, 1)
+
+    @pl.when(core == 1)
+    def _():
+        for l in range(depth):
+            pad(l, (tiles + 1, blocks + 1), tiles, blocks)
+
+    def energy_window(l, s, c):
+        own = EP[l, 1 + s]
+        if c == 0:
+            EV[l, s, c] = lane_rows(jnp.where(group == GROUPS - 1, EP[l, s], own), width)
+        else:
+            EV[l, s, c] = lane_rows(jnp.where(group == 0, EP[l, s + 2], own), -width)
+
+    late = ((0, 0), (blocks - 1, 1))
+    for l in range(depth):
+        for s in range(blocks):
+            for c in range(2):
+                if (s, c) not in late:
+                    energy_window(l, s, c)
+
+    senders = jnp.where(here, 2 * (n_az // n_rad - 1) + 1, 2 * (n_az // n_rad) + 1)
+    pl.semaphore_wait(barrier, senders)
+
+    swap_shift = remote(shifts, other, shift_sem.at[0], shift_sem.at[1], partner)
+    swap_shift.start()
+
+    def swaps(l, up):
+        src = (tiles, blocks) if up else (1, 1)
+        dst = (0, 0) if up else (tiles + 1, blocks + 1)
+        return [
+            remote(T4.at[l, src[0]], T4.at[l, dst[0]], swap_sem.at[0, l], swap_sem.at[1, l], partner),
+            remote(EP.at[l, src[1]], EP.at[l, dst[1]], swap_sem.at[2, l], swap_sem.at[3, l], partner),
+        ]
+
+    @pl.when(core == 0)
+    def _():
+        for l in range(depth):
+            for copy in swaps(l, True):
+                copy.start()
+
+    @pl.when(core == 1)
+    def _():
+        for l in range(depth):
+            for copy in swaps(l, False):
+                copy.start()
+
+    targets = [(ks, kl, kc) for ks in (2, 1, 3, 0) for kl in (1, 0) for kc in (1, 0)]
+
+    def target(ks, kl, kc):
+        s = lax.rem(block + ks, blocks)
+        l = lax.rem(layer + kl, depth)
+        c = lax.rem(core + kc, 2)
+        return s, l, c, {"az": (s * depth + l) * n_rad + core, "rad": c}
+
+    def send(kind, index):
+        ks, kl, kc = targets[index]
+        s, l, c, where = target(ks, kl, kc)
+        if kind == "own":
+            src, dst = T4.at[l, pl.ds(GROUPS * s + 1 + 2 * c, 2)], W4.at[me, pl.ds(1, 2)]
+            sems = own_send.at[index], own_recv.at[me]
+        elif kind == "side":
+            src, dst = T4.at[l, GROUPS * s + 5 * c], W4.at[me, 3 * c]
+            sems = side_send.at[index], side_recv.at[me]
+        else:
+            src, dst = EV.at[l, s, c], WE.at[me]
+            sems = last_send.at[index], last_recv.at[me]
+        across = remote(src, dst, *sems, where)
+        if (ks, kl, kc) != (0, 0, 0):
+            return across, None
+        return across, pltpu.make_async_copy(src, dst, sems[1])
+
+    def start(kind):
+        for index in range(len(targets)):
+            across, within = send(kind, index)
+            if within is None:
+                across.start()
+            else:
+
+                @pl.when(here)
+                def _():
+                    within.start()
+
+                @pl.when(jnp.logical_not(here))
+                def _():
+                    across.start()
+
+    def end(kind):
+        for index in range(len(targets)):
+            across, within = send(kind, index)
+            if within is None:
+                across.wait_send()
+            else:
+
+                @pl.when(jnp.logical_not(here))
+                def _():
+                    across.wait_send()
+
+    start("own")
+    for l in range(depth):
+        for copy in swaps(l, True):
+            copy.wait_recv()
+    start("side")
+    for l in range(depth):
+        for s, c in late:
+            energy_window(l, s, c)
+    start("last")
+
+    swap_shift.wait_recv()
+    first = jnp.full((1, lanes), core, jnp.int32) == 0
+    mine, theirs = shifts[...], other[...]
+    for c in range(2):
+        part = jnp.where(first, mine if c == 0 else theirs, theirs if c == 0 else mine)
+        table = jnp.broadcast_to(part.astype(jnp.float32), (lanes, lanes)).T.astype(jnp.int32)
+        SC[TILE + c * lanes : TILE + (c + 1) * lanes] = table
+    SC[0:TILE] = jnp.zeros((TILE, lanes), jnp.int32)
+    SC[TILE + 2 * lanes :] = jnp.zeros((TILE, lanes), jnp.int32)
+    amount = SC[pl.ds(pl.multiple_of(place * 2 * TILE, TILE), rows)]
+
+    def passes(i):
+        return remote(W4.at[i, 2 - core], W4.at[i, 3 * core], pass_send.at[i], pass_recv.at[i], partner)
+
+    def arrived(dst, recv):
+        return pltpu.make_async_copy(dst, dst, recv)
+
+    for k in range(n_az):
+        i = lax.rem(me + k, n_az)
+        arrived(W4.at[i, pl.ds(1, 2)], own_recv.at[i]).wait()
+        passes(i).start()
+
+    wide_lane = lax.broadcasted_iota(jnp.int32, (rows, lanes), 1)
+    source = (wide_lane - amount) & (lanes - 1)
+    inside = wide_lane >= amount
+
+    def rotate(field):
+        chunks = [field[:, v * lanes : (v + 1) * lanes] for v in range(GROUPS)]
+        turned = [jnp.take_along_axis(chunk, source, axis=1) for chunk in chunks]
+        return jnp.concatenate(
+            [jnp.where(inside, turned[v], turned[v - 1]) for v in range(GROUPS)], axis=1
+        )
+
+    total = GROUPS * lanes
+    at = jnp.full((TILE, total), place, jnp.int32)
+    lowest = at == 0
+    highest = at == 2 * blocks * n_rad - 1
+
+    def edged(field):
+        low = jnp.broadcast_to(field[TILE : TILE + 1], (TILE, total))
+        high = jnp.broadcast_to(field[3 * TILE - 1 : 3 * TILE], (TILE, total))
+        return jnp.concatenate(
+            [
+                jnp.where(lowest, low, field[:TILE]),
+                field[TILE : 3 * TILE],
+                jnp.where(highest, high, field[3 * TILE :]),
+            ],
+            axis=0,
+        )
+
+    for k in range(n_az):
+        i = lax.rem(me + k, n_az)
+        arrived(W4.at[i, 3 * core], side_recv.at[i]).wait()
+    for i in range(n_az):
+        passes(i).wait_recv()
+
+    columns = []
+    for v in range(GROUPS):
+        parts = [W4[GROUPS * v + b].reshape(rows, lanes) for b in range(GROUPS)]
+        columns.append(regroup(parts, wide_lane))
+    state = [edged(jnp.concatenate([columns[v][f] for v in range(GROUPS)], axis=1)) for f in range(4)]
+    step = advect_all(state)
+    state = [edged(rotate(step(field))) for field in state]
+
+    for k in range(n_az):
+        i = lax.rem(me + k, n_az)
+        arrived(WE.at[i], last_recv.at[i]).wait()
+    columns = [regroup([WE[GROUPS * v + b] for b in range(GROUPS)], lane) for v in range(GROUPS)]
+    field = jnp.concatenate(
+        [jnp.concatenate([columns[v][w] for v in range(GROUPS)], axis=1) for w in range(4)], axis=0
+    )
+    state.append(edged(rotate(step(edged(field)))))
+
+    mr, mp, en = push_all(state)
+    state = [edged(field) for field in (state[0], mr, mp, state[3], en)]
+    step = advect_all(state)
+
+    def back(kind, k):
+        i = lax.rem(me + k, n_az)
+        P, R = ((PA, RA), (PB, RB), (PE, RE))[kind]
+        src, dst = P.at[i], R.at[layer, block, core]
+        sems = back_send.at[kind, k], back_recv.at[kind, (layer * blocks + block) * 2 + core]
+        across = remote(src, dst, *sems, {"az": i, "rad": half})
+        return across, None if k else pltpu.make_async_copy(src, dst, sems[1])
+
+    def start_back(kind):
+        for k in [*range(1, n_az), 0]:
+            across, within = back(kind, k)
+            if within is None:
+                across.start()
+            else:
+
+                @pl.when(here)
+                def _():
+                    within.start()
+
+                @pl.when(jnp.logical_not(here))
+                def _():
+                    across.start()
+
+    def pack(P, fields2):
+        for v in range(GROUPS):
+            cut = slice(v * lanes, (v + 1) * lanes)
+            parts = [f[(1 + t) * TILE : (2 + t) * TILE, cut] for f in fields2 for t in range(2)]
+            for b, part in enumerate(regroup(parts, lane)):
+                P[GROUPS * v + b] = part
+
+    rho, mz = (edged(rotate(step(state[f]))) for f in (0, 3))
+    pack(PA, (rho, mz))
+    start_back(0)
+    mr, mp, en = (edged(rotate(step(state[f]))) for f in (1, 2, 4))
+    mr, mp, en = push_all((rho, mr, mp, mz, en))
+    pack(PB, (mr, mp))
+    start_back(1)
+    for v in range(GROUPS // 2):
+        cuts = [slice(u * lanes, (u + 1) * lanes) for u in (v, v + GROUPS // 2)]
+        parts = [en[(1 + t) * TILE : (2 + t) * TILE, cut] for cut in cuts for t in range(2)]
+        for b, part in enumerate(regroup(parts, lane)):
+            folded = fold(part, lane, row)
+            PE[GROUPS * v + b] = folded[: TILE // 2]
+            PE[GROUPS * (v + GROUPS // 2) + b] = folded[TILE // 2 :]
+    start_back(2)
+
+    def returned(kind, l, s, c):
+        R = (RA, RB, RE)[kind]
+        return arrived(R.at[l, s, c], back_recv.at[kind, (l * blocks + s) * 2 + c])
+
+    everyone = [(l, s, c) for l in range(depth) for s in range(blocks) for c in range(2)]
+    for kind in range(2):
+        for l, s, c in everyone:
+            returned(kind, l, s, c).wait()
+    for l in range(depth):
+        pieces = []
+        for s in range(blocks):
+            for c in range(2):
+                A, B = RA[l, s, c], RB[l, s, c]
+                for t in range(2):
+                    a = lane_rows(A, width if t == 0 else -width)
+                    b = lane_rows(B, width if t == 0 else -width)
+                    if t == 0:
+                        p, q, r, u = A, b, B, a
+                    else:
+                        p, q, r, u = a, B, b, A
+                    pieces.append(
+                        jnp.where(group < 2, jnp.where(group == 0, p, q), jnp.where(group == 2, r, u))
+                    )
+        block_out = jnp.concatenate(pieces, axis=0).T
+        for f in range(4):
+            out[f, l] = block_out[f * width : (f + 1) * width]
+    for l, s, c in everyone:
+        returned(2, l, s, c).wait()
+    pieces = []
+    for s in range(blocks):
+        both = [fold(jnp.concatenate([RE[l, s, 0], RE[l, s, 1]], axis=0), lane, row) for l in range(depth)]
+        for g in range(GROUPS):
+            piece = lane_rows(both[0], -width * g)
+            for l in range(1, depth):
+                piece = jnp.where(group == l, lane_rows(both[l], width * (l - g)), piece)
+            pieces.append(piece)
+    block_out = jnp.concatenate(pieces, axis=0).T
+    for l in range(depth):
+        out[4, l] = block_out[l * width : (l + 1) * width]
+
+    swap_shift.wait_send()
+    for l in range(depth):
+        for copy in swaps(l, True):
+            copy.wait_send()
+    for kind in ("own", "side", "last"):
+        end(kind)
+    for i in range(n_az):
+        passes(i).wait_send()
+    for kind in range(3):
+        for k in range(n_az):
+            across, within = back(kind, k)
+            if within is None:
+                across.wait_send()
+            else:
+
+                @pl.when(jnp.logical_not(here))
+                def _():
+                    across.wait_send()
+
+
+def turned_body(mesh, state, shifts):
+    n_az, n_rad = mesh.shape["az"], mesh.shape["rad"]
+    fields, depth, width, lanes = state.shape
+    blocks = n_az // (depth * n_rad)
+    tiles = lanes // TILE
+    vmem = lambda *shape: pltpu.VMEM(shape, jnp.float32)
+    dma = pltpu.SemaphoreType.DMA
+    tile = (TILE, lanes)
+    return pl.pallas_call(
+        functools.partial(turned_kernel, n_az, n_rad),
+        out_shape=pltpu.VMEM(state.shape, state.dtype),
+        in_specs=[pl.BlockSpec(memory_space=pl.ANY), pl.BlockSpec(memory_space=pltpu.VMEM)],
+        out_specs=pl.BlockSpec(memory_space=pltpu.VMEM),
+        scratch_shapes=[
+            vmem(fields, depth, width, lanes),
+            vmem(depth, tiles + 2, *tile),
+            vmem(depth, blocks + 2, *tile),
+            vmem(depth, blocks, 2, *tile),
+            vmem(n_az, 4, *tile),
+            vmem(n_az, *tile),
+            pltpu.VMEM((1, lanes), jnp.int32),
+            pltpu.VMEM((2 * lanes + 2 * TILE, lanes), jnp.int32),
+            vmem(n_az, *tile),
+            vmem(n_az, *tile),
+            vmem(n_az, TILE // 2, lanes),
+            vmem(depth, blocks, 2, *tile),
+            vmem(depth, blocks, 2, *tile),
+            vmem(depth, blocks, 2, TILE // 2, lanes),
+            dma((depth,)),
+            dma((2,)),
+            dma((4, depth)),
+            dma((n_az,)),
+            dma((n_az,)),
+            dma((n_az,)),
+            dma((n_az,)),
+            dma((n_az,)),
+            dma((n_az,)),
+            dma((n_az,)),
+            dma((n_az,)),
+            dma((3, n_az)),
+            dma((3, n_az)),
+        ],
+        compiler_params=pltpu.CompilerParams(collective_id=0, has_side_effects=True),
+    )(state, shifts.reshape(1, -1))
+
+
+def turns(mesh, state):
+    n_az, n_rad = mesh.shape["az"], mesh.shape["rad"]
+    fields, depth, width, lanes = state.shape
+    tiles = lanes // TILE
+    return (
+        n_rad == 2
+        and fields == GROUPS + 1
+        and width * GROUPS == lanes
+        and n_az == GROUPS * GROUPS
+        and n_az % (depth * n_rad) == 0
+        and tiles == GROUPS * (n_az // (depth * n_rad))
+        and depth * width <= lanes
+        and SMAX <= lanes
+    )
+
+
+def choose(mesh, state, shifts):
+    return (turned_body if turns(mesh, state) else body)(mesh, state, shifts)
+
+
 def solution(mesh):
     in_specs = (P(None, None, "az", "rad"), P("rad"))
     out_specs = P(None, None, "az", "rad")
     return jax.shard_map(
-        functools.partial(body, mesh), mesh=mesh, in_specs=in_specs, out_specs=out_specs, check_vma=False
+        functools.partial(choose, mesh), mesh=mesh, in_specs=in_specs, out_specs=out_specs, check_vma=False
     )

time: 36.4 us -> 26.4 us (0.73)
  Pallas kernels: 35.3 us -> 25.6 us
    pallas_call x1, Pallas kernels: 35.3 us -> 25.6 us  [turned_body(): pl.pallas_call(functools.partial(turned_kernel, n_az, n_rad), out_shape=p...]
where the time goes in v1:
time: 26.4 us; the launch traced here: 26.2 us
  Pallas kernels  25.6 us (97%)
  local copies, waits for them, and re-layouts  0.67 us (3%)
    pallas_call x1, Pallas kernels, turned_body(): pl.pallas_call(functools.partial(turned_kernel, n_az, n_rad), out_shape=p...  25.6 us
    unnamed x1, local copies, waits for them, and re-layouts  0.67 us

profile of v1, /device:TPU:0, one launch (start us, length us, event | category | flops | bytes accessed | tf_op | source)
XLA Modules:
  0.0 26.2 jit_solution(1233766427755293071)
XLA Ops:
  0.0 25.6 %shard_map.28 = f32[5,2,32,128]{3,2,1,0:T(8,128)S(1)} custom-call(f32[5,2,32,128]{3,2,1,0:T(8,128)} %x_in.1, s32[1,128]{1,0:T(1,128)} %bitcast.1), custom_call_target="tpu_custom_call" | custom-call | tf_op jit(solution)/shard_map/pallas_call | solution.py:745
  25.6 0.7 %copy.4 = f32[5,2,32,128]{3,2,1,0:T(8,128)} copy(f32[5,2,32,128]{3,2,1,0:T(8,128)S(1)} %shard_map.28) | data formatting | bytes 327680

commit v2 on v1

--- a/solution.py
+++ b/solution.py
@@ -628,26 +628,34 @@
     state = [edged(field) for field in (state[0], mr, mp, state[3], en)]
     step = advect_all(state)
 
-    def back(kind, k):
-        i = lax.rem(me + k, n_az)
+    plane = n_az // GROUPS
+    order = [(q, j) for q in range(GROUPS) for j in [*range(1, plane), 0]]
+
+    def back(kind, q, j):
+        i = q * plane + lax.rem(me + j, plane)
         P, R = ((PA, RA), (PB, RB), (PE, RE))[kind]
         src, dst = P.at[i], R.at[layer, block, core]
-        sems = back_send.at[kind, k], back_recv.at[kind, (layer * blocks + block) * 2 + core]
+        sems = back_send.at[kind, q * plane + j], back_recv.at[kind, (layer * blocks + block) * 2 + core]
         across = remote(src, dst, *sems, {"az": i, "rad": half})
-        return across, None if k else pltpu.make_async_copy(src, dst, sems[1])
-
-    def start_back(kind):
-        for k in [*range(1, n_az), 0]:
-            across, within = back(kind, k)
+        return across, None if j else pltpu.make_async_copy(src, dst, sems[1])
+
+    def stays(q):
+        return jnp.logical_and(here, me // plane == q)
+
+    def start_back(kind, q):
+        for at_q, j in order:
+            if at_q != q:
+                continue
+            across, within = back(kind, q, j)
             if within is None:
                 across.start()
             else:
 
-                @pl.when(here)
+                @pl.when(stays(q))
                 def _():
                     within.start()
 
-                @pl.when(jnp.logical_not(here))
+                @pl.when(jnp.logical_not(stays(q)))
                 def _():
                     across.start()
 
@@ -660,11 +668,11 @@
 
     rho, mz = (edged(rotate(step(state[f]))) for f in (0, 3))
     pack(PA, (rho, mz))
-    start_back(0)
+    for q in range(GROUPS):
+        start_back(0, q)
     mr, mp, en = (edged(rotate(step(state[f]))) for f in (1, 2, 4))
     mr, mp, en = push_all((rho, mr, mp, mz, en))
     pack(PB, (mr, mp))
-    start_back(1)
     for v in range(GROUPS // 2):
         cuts = [slice(u * lanes, (u + 1) * lanes) for u in (v, v + GROUPS // 2)]
         parts = [en[(1 + t) * TILE : (2 + t) * TILE, cut] for cut in cuts for t in range(2)]
@@ -672,7 +680,9 @@
             folded = fold(part, lane, row)
             PE[GROUPS * v + b] = folded[: TILE // 2]
             PE[GROUPS * (v + GROUPS // 2) + b] = folded[TILE // 2 :]
-    start_back(2)
+    for q in range(GROUPS):
+        start_back(1, q)
+        start_back(2, q)
 
     def returned(kind, l, s, c):
         R = (RA, RB, RE)[kind]
@@ -723,13 +733,13 @@
     for i in range(n_az):
         passes(i).wait_send()
     for kind in range(3):
-        for k in range(n_az):
-            across, within = back(kind, k)
+        for q, j in order:
+            across, within = back(kind, q, j)
             if within is None:
                 across.wait_send()
             else:
 
-                @pl.when(jnp.logical_not(here))
+                @pl.when(jnp.logical_not(stays(q)))
                 def _():
                     across.wait_send()
 

time: 26.4 us -> 26.5 us (level)
  no operation moved by 1% of the time
where the time goes in v2:
time: 26.5 us; the launch traced here: 26.3 us
  Pallas kernels  25.6 us (97%)
  local copies, waits for them, and re-layouts  0.67 us (3%)
    pallas_call x1, Pallas kernels, turned_body(): pl.pallas_call(functools.partial(turned_kernel, n_az, n_rad), out_shape=p...  25.6 us
    unnamed x1, local copies, waits for them, and re-layouts  0.67 us

profile of v2, /device:TPU:0, one launch (start us, length us, event | category | flops | bytes accessed | tf_op | source)
XLA Modules:
  0.0 26.3 jit_solution(9650808334170144946)
XLA Ops:
  0.0 25.6 %shard_map.28 = f32[5,2,32,128]{3,2,1,0:T(8,128)S(1)} custom-call(f32[5,2,32,128]{3,2,1,0:T(8,128)} %x_in.1, s32[1,128]{1,0:T(1,128)} %bitcast.1), custom_call_target="tpu_custom_call" | custom-call | tf_op jit(solution)/shard_map/pallas_call | solution.py:755
  25.6 0.7 %copy.4 = f32[5,2,32,128]{3,2,1,0:T(8,128)} copy(f32[5,2,32,128]{3,2,1,0:T(8,128)S(1)} %shard_map.28) | data formatting | bytes 327680

commit v3 on v1

--- a/solution.py
+++ b/solution.py
@@ -389,8 +389,8 @@
 
 
 def turned_kernel(n_az, n_rad, x_in, shifts, out, *scratch):
-    (x, T4, EP, EV, W4, WE, other, SC, PA, PB, PE, RA, RB, RE, load_sem, shift_sem, swap_sem, own_send, own_recv,
-     side_send, side_recv, last_send, last_recv, pass_send, pass_recv, back_send, back_recv) = scratch
+    (x, T4, EP, M, W, other, SC, B, R, load_sem, shift_sem, swap_sem, out_send, out_recv, pass_send, pass_recv,
+     back_send, back_recv) = scratch
     fields, depth, width, lanes = x.shape
     blocks = n_az // (depth * n_rad)
     tiles = lanes // TILE
@@ -450,19 +450,21 @@
         for l in range(depth):
             pad(l, (tiles + 1, blocks + 1), tiles, blocks)
 
-    def energy_window(l, s, c):
+    def stage(l, s, c):
         own = EP[l, 1 + s]
         if c == 0:
-            EV[l, s, c] = lane_rows(jnp.where(group == GROUPS - 1, EP[l, s], own), width)
+            M[l, s, c, 0] = lane_rows(jnp.where(group == GROUPS - 1, EP[l, s], own), width)
+            M[l, s, c, 1:4] = T4[l, GROUPS * s : GROUPS * s + 3]
         else:
-            EV[l, s, c] = lane_rows(jnp.where(group == 0, EP[l, s + 2], own), -width)
+            M[l, s, c, 0:3] = T4[l, GROUPS * s + 3 : GROUPS * s + 6]
+            M[l, s, c, 3] = lane_rows(jnp.where(group == 0, EP[l, s + 2], own), -width)
 
     late = ((0, 0), (blocks - 1, 1))
     for l in range(depth):
         for s in range(blocks):
             for c in range(2):
                 if (s, c) not in late:
-                    energy_window(l, s, c)
+                    stage(l, s, c)
 
     senders = jnp.where(here, 2 * (n_az // n_rad - 1) + 1, 2 * (n_az // n_rad) + 1)
     pl.semaphore_wait(barrier, senders)
@@ -490,88 +492,80 @@
             for copy in swaps(l, False):
                 copy.start()
 
-    targets = [(ks, kl, kc) for ks in (2, 1, 3, 0) for kl in (1, 0) for kc in (1, 0)]
-
-    def target(ks, kl, kc):
+    targets = [(ks, kl, kc) for ks in (2, 1, 3, 0) for kl in range(depth) for kc in (1, 0)]
+
+    def send(index):
+        ks, kl, kc = targets[index]
         s = lax.rem(block + ks, blocks)
         l = lax.rem(layer + kl, depth)
         c = lax.rem(core + kc, 2)
-        return s, l, c, {"az": (s * depth + l) * n_rad + core, "rad": c}
-
-    def send(kind, index):
-        ks, kl, kc = targets[index]
-        s, l, c, where = target(ks, kl, kc)
-        if kind == "own":
-            src, dst = T4.at[l, pl.ds(GROUPS * s + 1 + 2 * c, 2)], W4.at[me, pl.ds(1, 2)]
-            sems = own_send.at[index], own_recv.at[me]
-        elif kind == "side":
-            src, dst = T4.at[l, GROUPS * s + 5 * c], W4.at[me, 3 * c]
-            sems = side_send.at[index], side_recv.at[me]
-        else:
-            src, dst = EV.at[l, s, c], WE.at[me]
-            sems = last_send.at[index], last_recv.at[me]
-        across = remote(src, dst, *sems, where)
-        if (ks, kl, kc) != (0, 0, 0):
-            return across, None
-        return across, pltpu.make_async_copy(src, dst, sems[1])
-
-    def start(kind):
+        src, dst = M.at[l, s, c], W.at[me, pl.ds(c, 4)]
+        sems = out_send.at[index], out_recv.at[me]
+        across = remote(src, dst, *sems, {"az": (s * depth + l) * n_rad + core, "rad": c})
+        is_late = s == c * (blocks - 1)
+        return across, None if ks or kl or kc else pltpu.make_async_copy(src, dst, sems[1]), is_late
+
+    def start(want_late):
         for index in range(len(targets)):
-            across, within = send(kind, index)
+            across, within, is_late = send(index)
+            now = is_late if want_late else jnp.logical_not(is_late)
             if within is None:
-                across.start()
+
+                @pl.when(now)
+                def _():
+                    across.start()
+
             else:
 
-                @pl.when(here)
+                @pl.when(jnp.logical_and(now, here))
                 def _():
                     within.start()
 
-                @pl.when(jnp.logical_not(here))
+                @pl.when(jnp.logical_and(now, jnp.logical_not(here)))
                 def _():
                     across.start()
 
-    def end(kind):
-        for index in range(len(targets)):
-            across, within = send(kind, index)
-            if within is None:
-                across.wait_send()
-            else:
-
-                @pl.when(jnp.logical_not(here))
-                def _():
-                    across.wait_send()
-
-    start("own")
+    start(False)
     for l in range(depth):
         for copy in swaps(l, True):
             copy.wait_recv()
-    start("side")
     for l in range(depth):
         for s, c in late:
-            energy_window(l, s, c)
-    start("last")
+            stage(l, s, c)
+    start(True)
 
     swap_shift.wait_recv()
-    first = jnp.full((1, lanes), core, jnp.int32) == 0
+    lower = jnp.full((1, lanes), core, jnp.int32) == 0
     mine, theirs = shifts[...], other[...]
     for c in range(2):
-        part = jnp.where(first, mine if c == 0 else theirs, theirs if c == 0 else mine)
+        part = jnp.where(lower, mine if c == 0 else theirs, theirs if c == 0 else mine)
         table = jnp.broadcast_to(part.astype(jnp.float32), (lanes, lanes)).T.astype(jnp.int32)
         SC[TILE + c * lanes : TILE + (c + 1) * lanes] = table
     SC[0:TILE] = jnp.zeros((TILE, lanes), jnp.int32)
     SC[TILE + 2 * lanes :] = jnp.zeros((TILE, lanes), jnp.int32)
     amount = SC[pl.ds(pl.multiple_of(place * 2 * TILE, TILE), rows)]
 
-    def passes(i):
-        return remote(W4.at[i, 2 - core], W4.at[i, 3 * core], pass_send.at[i], pass_recv.at[i], partner)
+    plane = n_az // GROUPS
+    near = [lax.rem(me // plane + k, GROUPS) for k in (0, 1, 3, 2)]
+
+    def passes(k):
+        ahead = pl.ds(near[k] * plane, plane)
+        return remote(W.at[ahead, 3 - 2 * core], W.at[ahead, 4 * core], pass_send.at[k], pass_recv.at[near[k]], partner)
+
+    def passed(q):
+        return remote(
+            W.at[pl.ds(q * plane, plane), 3 - 2 * core], W.at[pl.ds(q * plane, plane), 4 - 4 * core],
+            pass_send.at[q], pass_recv.at[q], partner
+        )
 
     def arrived(dst, recv):
         return pltpu.make_async_copy(dst, dst, recv)
 
-    for k in range(n_az):
-        i = lax.rem(me + k, n_az)
-        arrived(W4.at[i, pl.ds(1, 2)], own_recv.at[i]).wait()
-        passes(i).start()
+    for k in range(GROUPS):
+        for j in range(plane):
+            i = near[k] * plane + lax.rem(me + j, plane)
+            arrived(W.at[i, pl.ds(core, 4)], out_recv.at[i]).wait()
+        passes(k).start()
 
     wide_lane = lax.broadcasted_iota(jnp.int32, (rows, lanes), 1)
     source = (wide_lane - amount) & (lanes - 1)
@@ -601,24 +595,18 @@
             axis=0,
         )
 
-    for k in range(n_az):
-        i = lax.rem(me + k, n_az)
-        arrived(W4.at[i, 3 * core], side_recv.at[i]).wait()
-    for i in range(n_az):
-        passes(i).wait_recv()
+    for q in range(GROUPS):
+        passed(q).wait_recv()
 
     columns = []
     for v in range(GROUPS):
-        parts = [W4[GROUPS * v + b].reshape(rows, lanes) for b in range(GROUPS)]
+        parts = [W[GROUPS * v + b, pl.ds(1 - core, 4)].reshape(rows, lanes) for b in range(GROUPS)]
         columns.append(regroup(parts, wide_lane))
     state = [edged(jnp.concatenate([columns[v][f] for v in range(GROUPS)], axis=1)) for f in range(4)]
     step = advect_all(state)
     state = [edged(rotate(step(field))) for field in state]
 
-    for k in range(n_az):
-        i = lax.rem(me + k, n_az)
-        arrived(WE.at[i], last_recv.at[i]).wait()
-    columns = [regroup([WE[GROUPS * v + b] for b in range(GROUPS)], lane) for v in range(GROUPS)]
+    columns = [regroup([W[GROUPS * v + b, 4 * core] for b in range(GROUPS)], lane) for v in range(GROUPS)]
     field = jnp.concatenate(
         [jnp.concatenate([columns[v][w] for v in range(GROUPS)], axis=1) for w in range(4)], axis=0
     )
@@ -628,83 +616,74 @@
     state = [edged(field) for field in (state[0], mr, mp, state[3], en)]
     step = advect_all(state)
 
-    def back(kind, k):
-        i = lax.rem(me + k, n_az)
-        P, R = ((PA, RA), (PB, RB), (PE, RE))[kind]
-        src, dst = P.at[i], R.at[layer, block, core]
-        sems = back_send.at[kind, k], back_recv.at[kind, (layer * blocks + block) * 2 + core]
+    order = [(k, j) for k in (2, 1, 3, 0) for j in [*range(1, plane), 0]]
+
+    def back(index):
+        k, j = order[index]
+        i = lax.rem(me // plane + k, GROUPS) * plane + lax.rem(me + j, plane)
+        src, dst = B.at[i], R.at[layer, block, core]
+        sems = back_send.at[index], back_recv.at[(layer * blocks + block) * 2 + core]
         across = remote(src, dst, *sems, {"az": i, "rad": half})
-        return across, None if k else pltpu.make_async_copy(src, dst, sems[1])
-
-    def start_back(kind):
-        for k in [*range(1, n_az), 0]:
-            across, within = back(kind, k)
-            if within is None:
-                across.start()
-            else:
-
-                @pl.when(here)
-                def _():
-                    within.start()
-
-                @pl.when(jnp.logical_not(here))
-                def _():
-                    across.start()
-
-    def pack(P, fields2):
+        return across, None if k or j else pltpu.make_async_copy(src, dst, sems[1])
+
+    def pack(to, fields2):
         for v in range(GROUPS):
             cut = slice(v * lanes, (v + 1) * lanes)
             parts = [f[(1 + t) * TILE : (2 + t) * TILE, cut] for f in fields2 for t in range(2)]
             for b, part in enumerate(regroup(parts, lane)):
-                P[GROUPS * v + b] = part
+                B[GROUPS * v + b, to * TILE : (to + 1) * TILE] = part
 
     rho, mz = (edged(rotate(step(state[f]))) for f in (0, 3))
-    pack(PA, (rho, mz))
-    start_back(0)
+    pack(0, (rho, mz))
     mr, mp, en = (edged(rotate(step(state[f]))) for f in (1, 2, 4))
     mr, mp, en = push_all((rho, mr, mp, mz, en))
-    pack(PB, (mr, mp))
-    start_back(1)
+    pack(1, (mr, mp))
     for v in range(GROUPS // 2):
         cuts = [slice(u * lanes, (u + 1) * lanes) for u in (v, v + GROUPS // 2)]
         parts = [en[(1 + t) * TILE : (2 + t) * TILE, cut] for cut in cuts for t in range(2)]
         for b, part in enumerate(regroup(parts, lane)):
             folded = fold(part, lane, row)
-            PE[GROUPS * v + b] = folded[: TILE // 2]
-            PE[GROUPS * (v + GROUPS // 2) + b] = folded[TILE // 2 :]
-    start_back(2)
-
-    def returned(kind, l, s, c):
-        R = (RA, RB, RE)[kind]
-        return arrived(R.at[l, s, c], back_recv.at[kind, (l * blocks + s) * 2 + c])
-
-    everyone = [(l, s, c) for l in range(depth) for s in range(blocks) for c in range(2)]
-    for kind in range(2):
-        for l, s, c in everyone:
-            returned(kind, l, s, c).wait()
+            B[GROUPS * v + b, 2 * TILE :] = folded[: TILE // 2]
+            B[GROUPS * (v + GROUPS // 2) + b, 2 * TILE :] = folded[TILE // 2 :]
+    for index in range(len(order)):
+        across, within = back(index)
+        if within is None:
+            across.start()
+        else:
+
+            @pl.when(here)
+            def _():
+                within.start()
+
+            @pl.when(jnp.logical_not(here))
+            def _():
+                across.start()
+
+    for l in range(depth):
+        for s in range(blocks):
+            for c in range(2):
+                arrived(R.at[l, s, c], back_recv.at[(l * blocks + s) * 2 + c]).wait()
     for l in range(depth):
         pieces = []
         for s in range(blocks):
             for c in range(2):
-                A, B = RA[l, s, c], RB[l, s, c]
+                first, second = R[l, s, c, :TILE], R[l, s, c, TILE : 2 * TILE]
                 for t in range(2):
-                    a = lane_rows(A, width if t == 0 else -width)
-                    b = lane_rows(B, width if t == 0 else -width)
+                    a = lane_rows(first, width if t == 0 else -width)
+                    b = lane_rows(second, width if t == 0 else -width)
                     if t == 0:
-                        p, q, r, u = A, b, B, a
+                        p, q, r, u = first, b, second, a
                     else:
-                        p, q, r, u = a, B, b, A
+                        p, q, r, u = a, second, b, first
                     pieces.append(
                         jnp.where(group < 2, jnp.where(group == 0, p, q), jnp.where(group == 2, r, u))
                     )
         block_out = jnp.concatenate(pieces, axis=0).T
         for f in range(4):
             out[f, l] = block_out[f * width : (f + 1) * width]
-    for l, s, c in everyone:
-        returned(2, l, s, c).wait()
     pieces = []
     for s in range(blocks):
-        both = [fold(jnp.concatenate([RE[l, s, 0], RE[l, s, 1]], axis=0), lane, row) for l in range(depth)]
+        both = [fold(jnp.concatenate([R[l, s, c, 2 * TILE :] for c in range(2)], axis=0), lane, row) for l in range(depth)]
         for g in range(GROUPS):
             piece = lane_rows(both[0], -width * g)
             for l in range(1, depth):
@@ -718,20 +697,27 @@
     for l in range(depth):
         for copy in swaps(l, True):
             copy.wait_send()
-    for kind in ("own", "side", "last"):
-        end(kind)
-    for i in range(n_az):
-        passes(i).wait_send()
-    for kind in range(3):
-        for k in range(n_az):
-            across, within = back(kind, k)
-            if within is None:
+    for index in range(len(targets)):
+        across, within, _ = send(index)
+        if within is None:
+            across.wait_send()
+        else:
+
+            @pl.when(jnp.logical_not(here))
+            def _():
                 across.wait_send()
-            else:
-
-                @pl.when(jnp.logical_not(here))
-                def _():
-                    across.wait_send()
+
+    for k in range(GROUPS):
+        passes(k).wait_send()
+    for index in range(len(order)):
+        across, within = back(index)
+        if within is None:
+            across.wait_send()
+        else:
+
+            @pl.when(jnp.logical_not(here))
+            def _():
+                across.wait_send()
 
 
 def turned_body(mesh, state, shifts):
@@ -751,30 +737,21 @@
             vmem(fields, depth, width, lanes),
             vmem(depth, tiles + 2, *tile),
             vmem(depth, blocks + 2, *tile),
-            vmem(depth, blocks, 2, *tile),
-            vmem(n_az, 4, *tile),
-            vmem(n_az, *tile),
+            vmem(depth, blocks, 2, 4, *tile),
+            vmem(n_az, 5, *tile),
             pltpu.VMEM((1, lanes), jnp.int32),
             pltpu.VMEM((2 * lanes + 2 * TILE, lanes), jnp.int32),
-            vmem(n_az, *tile),
-            vmem(n_az, *tile),
-            vmem(n_az, TILE // 2, lanes),
-            vmem(depth, blocks, 2, *tile),
-            vmem(depth, blocks, 2, *tile),
-            vmem(depth, blocks, 2, TILE // 2, lanes),
+            vmem(n_az, 2 * TILE + TILE // 2, lanes),
+            vmem(depth, blocks, 2, 2 * TILE + TILE // 2, lanes),
             dma((depth,)),
             dma((2,)),
             dma((4, depth)),
             dma((n_az,)),
             dma((n_az,)),
+            dma((GROUPS,)),
+            dma((GROUPS,)),
             dma((n_az,)),
             dma((n_az,)),
-            dma((n_az,)),
-            dma((n_az,)),
-            dma((n_az,)),
-            dma((n_az,)),
-            dma((3, n_az)),
-            dma((3, n_az)),
         ],
         compiler_params=pltpu.CompilerParams(collective_id=0, has_side_effects=True),
     )(state, shifts.reshape(1, -1))

time: 26.4 us -> 27.6 us (1.045)
  Pallas kernels: 25.6 us -> 26.8 us
    pallas_call x1, Pallas kernels: 25.6 us -> 26.8 us  [turned_body(): pl.pallas_call(functools.partial(turned_kernel, n_az, n_rad), out_shape=p...]
where the time goes in v3:
time: 27.6 us; the launch traced here: 27.4 us
  Pallas kernels  26.8 us (97%)
  local copies, waits for them, and re-layouts  0.67 us (2%)
    pallas_call x1, Pallas kernels, turned_body(): pl.pallas_call(functools.partial(turned_kernel, n_az, n_rad), out_shape=p...  26.8 us
    unnamed x1, local copies, waits for them, and re-layouts  0.67 us

profile of v3, /device:TPU:0, one launch (start us, length us, event | category | flops | bytes accessed | tf_op | source)
XLA Modules:
  0.0 27.4 jit_solution(2146122291490699638)
XLA Ops:
  0.0 26.8 %shard_map.28 = f32[5,2,32,128]{3,2,1,0:T(8,128)S(1)} custom-call(f32[5,2,32,128]{3,2,1,0:T(8,128)} %x_in.1, s32[1,128]{1,0:T(1,128)} %bitcast.1), custom_call_target="tpu_custom_call" | custom-call | tf_op jit(solution)/shard_map/pallas_call | solution.py:731
  26.8 0.7 %copy.4 = f32[5,2,32,128]{3,2,1,0:T(8,128)} copy(f32[5,2,32,128]{3,2,1,0:T(8,128)S(1)} %shard_map.28) | data formatting | bytes 327680

commit v4 on v3

--- a/solution.py
+++ b/solution.py
@@ -344,20 +344,12 @@
     return pltpu.roll(x, shift % x.shape[1], 1)
 
 
-def regroup(parts, lane):
-    size = parts[0].shape[1] // GROUPS
-    low = (lane & (2 * size)) == 0
-    even = (lane & size) == 0
-    a = [None] * GROUPS
-    for g in range(2):
-        p, q = parts[g], parts[g + 2]
-        a[g] = jnp.where(low, p, lane_rows(q, 2 * size))
-        a[g + 2] = jnp.where(low, lane_rows(p, 2 * size), q)
-    out = []
-    for g in (0, 2):
-        p, q = a[g], a[g + 1]
-        out.append(jnp.where(even, p, lane_rows(q, size)))
-        out.append(jnp.where(even, lane_rows(p, -size), q))
+def exchange(parts, lane):
+    n = len(parts)
+    out = [parts[-g % n] for g in range(n)]
+    for bit in range(n.bit_length() - 1):
+        far = (lane & (TILE << bit)) != 0
+        out = [jnp.where(far, out[(g - (1 << bit)) % n], out[g]) for g in range(n)]
     return out
 
 
@@ -367,29 +359,98 @@
     return jnp.where(stay, x, lane_rows(pltpu.roll(x, TILE // 2, 0), half))
 
 
+def line(tiles):
+    return jnp.concatenate(tiles, axis=0)
+
+
+def tiles_of(x):
+    return [x[g * TILE : (g + 1) * TILE] for g in range(GROUPS)]
+
+
+def next_of(x, axis):
+    first = x[:TILE]
+    return jnp.concatenate([x[TILE:], pltpu.roll(first, first.shape[axis] - 1, axis)], axis=0)
+
+
+def last_of(x, axis):
+    last = x[-TILE:]
+    return jnp.concatenate([pltpu.roll(last, 1, axis), x[:-TILE]], axis=0)
+
+
+def along(field, w):
+    return line([field[u][w] for u in range(GROUPS)])
+
+
+def across(field, u):
+    return line(field[u])
+
+
+def line_speeds(velocity, axis, courant):
+    face = (0.5 * courant) * (velocity + next_of(velocity, axis))
+    return jnp.maximum(face, 0.0), jnp.minimum(face, 0.0)
+
+
+def line_advect(field, speeds, axis):
+    low = field - last_of(field, axis)
+    high = next_of(low, axis)
+    product = low * high
+    half = jnp.where(product > 0, product / (low + high), 0.0)
+    flux = speeds[0] * (field + half) + speeds[1] * next_of(field - half, axis)
+    return flux - last_of(flux, axis)
+
+
+def line_push(pressure, density, speed, axis, courant):
+    compress = jnp.minimum(next_of(speed, axis) - last_of(speed, axis), 0.0)
+    total = pressure + VISCOSITY_COEF * density * compress * compress
+    work = total * speed
+    scale = -0.5 * courant
+    return scale * (next_of(total, axis) - last_of(total, axis)), scale * (next_of(work, axis) - last_of(work, axis))
+
+
 def advect_all(state):
-    rho, mr, mp = state[0], state[1], state[2]
-    inverse = 1.0 / rho
-    az_speeds = face_speeds(mp * inverse, 1, COURANT_AZIMUTH)
-    rad_speeds = face_speeds(mr * inverse, 0, COURANT_RADIAL)
+    rho, mr, mp = state[:3]
+    az_speeds, rad_speeds = [], []
+    inverse = [tiles_of(1.0 / across(rho, u)) for u in range(GROUPS)]
+    for g in range(GROUPS):
+        az_speeds.append(line_speeds(along(mp, g) * along(inverse, g), 1, COURANT_AZIMUTH))
+        rad_speeds.append(line_speeds(across(mr, g) * across(inverse, g), 0, COURANT_RADIAL))
 
     def step(field):
-        return field - advect(field, az_speeds, 1) - advect(field, rad_speeds, 0)
+        turned = [along(field, w) for w in range(GROUPS)]
+        turned = [tiles_of(turned[w] - line_advect(turned[w], az_speeds[w], 1)) for w in range(GROUPS)]
+        out = []
+        for u in range(GROUPS):
+            rest = line([turned[w][u] for w in range(GROUPS)])
+            out.append(tiles_of(rest - line_advect(across(field, u), rad_speeds[u], 0)))
+        return out
 
     return step
 
 
 def push_all(state):
     rho, mr, mp, mz, energy = state
-    inverse = 1.0 / rho
-    pressure = (GAMMA_GAS - 1.0) * (energy - 0.5 * (mr * mr + mp * mp + mz * mz) * inverse)
-    az_m, az_e = push(pressure, rho, mp * inverse, 1, COURANT_AZIMUTH)
-    rad_m, rad_e = push(pressure, rho, mr * inverse, 0, COURANT_RADIAL)
-    return mr + rad_m, mp + az_m, energy + az_e + rad_e
+    inverse, pressure, new_mr, rest = [], [], [], []
+    for u in range(GROUPS):
+        r, a, b, c, e = (across(f, u) for f in state)
+        inv = 1.0 / r
+        p = (GAMMA_GAS - 1.0) * (e - 0.5 * (a * a + b * b + c * c) * inv)
+        rad_m, rad_e = line_push(p, r, a * inv, 0, COURANT_RADIAL)
+        inverse.append(tiles_of(inv))
+        pressure.append(tiles_of(p))
+        new_mr.append(tiles_of(a + rad_m))
+        rest.append(tiles_of(e + rad_e))
+    new_mp = [[None] * GROUPS for _ in range(GROUPS)]
+    new_energy = [[None] * GROUPS for _ in range(GROUPS)]
+    for w in range(GROUPS):
+        b = along(mp, w)
+        az_m, az_e = line_push(along(pressure, w), along(rho, w), b * along(inverse, w), 1, COURANT_AZIMUTH)
+        for u, (m, e) in enumerate(zip(tiles_of(b + az_m), tiles_of(along(rest, w) + az_e))):
+            new_mp[u][w], new_energy[u][w] = m, e
+    return new_mr, new_mp, new_energy
 
 
 def turned_kernel(n_az, n_rad, x_in, shifts, out, *scratch):
-    (x, T4, EP, M, W, other, SC, B, R, load_sem, shift_sem, swap_sem, out_send, out_recv, pass_send, pass_recv,
+    (x, T4, EP, M, W, other, SC, AM, F, G, B, R, load_sem, shift_sem, swap_sem, out_send, out_recv, pass_send, pass_recv,
      back_send, back_recv) = scratch
     fields, depth, width, lanes = x.shape
     blocks = n_az // (depth * n_rad)
@@ -424,11 +485,17 @@
     row = lax.broadcasted_iota(jnp.int32, (TILE, lanes), 0)
     group = lane // width
 
+    spin = me * TILE
+
+    def rows_of(f, l):
+        return [x[f, l, pl.ds(u, width // GROUPS, stride=GROUPS), :] for u in range(GROUPS)]
+
     for l in range(depth):
         loads[l].wait()
-        T4[l, 1 : tiles + 1] = x[0:4, l].reshape(4 * width, lanes).T.reshape(tiles, TILE, lanes)
-    energy = x[4].reshape(depth * width, lanes)
-    turned = jnp.concatenate([energy] * (lanes // (depth * width)), axis=0).T.reshape(tiles, TILE, lanes)
+        cells = jnp.concatenate([part for f in range(GROUPS) for part in rows_of(f, l)], axis=0)
+        T4[l, 1 : tiles + 1] = pltpu.roll(cells.T, spin, 1).reshape(tiles, TILE, lanes)
+    energy = [part for l in range(depth) for part in rows_of(4, l)]
+    turned = jnp.concatenate(energy * (lanes // (depth * width)), axis=0).T.reshape(tiles, TILE, lanes)
     for l in range(depth):
         for m in range(tiles // GROUPS):
             packed = turned[GROUPS * m] if l == 0 else lane_rows(turned[GROUPS * m], -width * l)
@@ -436,28 +503,26 @@
                 packed = jnp.where(group == g, lane_rows(turned[GROUPS * m + g], width * (g - l)), packed)
             EP[l, 1 + m] = packed
 
-    def pad(l, to, tile_from, energy_from):
-        T4[l, to[0]] = T4[l, tile_from]
-        EP[l, to[1]] = EP[l, energy_from]
-
     @pl.when(core == 0)
     def _():
         for l in range(depth):
-            pad(l, (0, 0), 1, 1)
+            T4[l, 0] = jnp.broadcast_to(T4[l, 1, 0:1], (TILE, lanes))
+            EP[l, 0] = jnp.broadcast_to(lane_rows(EP[l, 1], -width)[0:1], (TILE, lanes))
 
     @pl.when(core == 1)
     def _():
         for l in range(depth):
-            pad(l, (tiles + 1, blocks + 1), tiles, blocks)
+            T4[l, tiles + 1] = jnp.broadcast_to(T4[l, tiles, TILE - 1 : TILE], (TILE, lanes))
+            EP[l, blocks + 1] = jnp.broadcast_to(lane_rows(EP[l, blocks], width)[TILE - 1 : TILE], (TILE, lanes))
 
     def stage(l, s, c):
         own = EP[l, 1 + s]
         if c == 0:
-            M[l, s, c, 0] = lane_rows(jnp.where(group == GROUPS - 1, EP[l, s], own), width)
+            M[l, s, c, 0] = pltpu.roll(jnp.where(group == GROUPS - 1, EP[l, s], own), lax.rem(spin + width, lanes), 1)
             M[l, s, c, 1:4] = T4[l, GROUPS * s : GROUPS * s + 3]
         else:
             M[l, s, c, 0:3] = T4[l, GROUPS * s + 3 : GROUPS * s + 6]
-            M[l, s, c, 3] = lane_rows(jnp.where(group == 0, EP[l, s + 2], own), -width)
+            M[l, s, c, 3] = pltpu.roll(jnp.where(group == 0, EP[l, s + 2], own), lax.rem(spin + lanes - width, lanes), 1)
 
     late = ((0, 0), (blocks - 1, 1))
     for l in range(depth):
@@ -501,19 +566,19 @@
         c = lax.rem(core + kc, 2)
         src, dst = M.at[l, s, c], W.at[me, pl.ds(c, 4)]
         sems = out_send.at[index], out_recv.at[me]
-        across = remote(src, dst, *sems, {"az": (s * depth + l) * n_rad + core, "rad": c})
+        sent = remote(src, dst, *sems, {"az": (s * depth + l) * n_rad + core, "rad": c})
         is_late = s == c * (blocks - 1)
-        return across, None if ks or kl or kc else pltpu.make_async_copy(src, dst, sems[1]), is_late
+        return sent, None if ks or kl or kc else pltpu.make_async_copy(src, dst, sems[1]), is_late
 
     def start(want_late):
         for index in range(len(targets)):
-            across, within, is_late = send(index)
+            sent, within, is_late = send(index)
             now = is_late if want_late else jnp.logical_not(is_late)
             if within is None:
 
                 @pl.when(now)
                 def _():
-                    across.start()
+                    sent.start()
 
             else:
 
@@ -523,7 +588,7 @@
 
                 @pl.when(jnp.logical_and(now, jnp.logical_not(here)))
                 def _():
-                    across.start()
+                    sent.start()
 
     start(False)
     for l in range(depth):
@@ -543,7 +608,15 @@
         SC[TILE + c * lanes : TILE + (c + 1) * lanes] = table
     SC[0:TILE] = jnp.zeros((TILE, lanes), jnp.int32)
     SC[TILE + 2 * lanes :] = jnp.zeros((TILE, lanes), jnp.int32)
-    amount = SC[pl.ds(pl.multiple_of(place * 2 * TILE, TILE), rows)]
+    AM[...] = SC[pl.ds(pl.multiple_of(place * 2 * TILE, TILE), rows)]
+    amounts = [AM[pl.ds(w, TILE, stride=GROUPS), :] for w in range(GROUPS)]
+    coarse = [amount // GROUPS for amount in amounts]
+    odd = [(amount & 1) != 0 for amount in amounts]
+    two = [(amount & 2) != 0 for amount in amounts]
+    source = [
+        [(lane - coarse[w] - jnp.where(u < (amounts[w] & (GROUPS - 1)), 1, 0)) & (lanes - 1) for w in range(GROUPS)]
+        for u in range(GROUPS)
+    ]
 
     plane = n_az // GROUPS
     near = [lax.rem(me // plane + k, GROUPS) for k in (0, 1, 3, 2)]
@@ -567,54 +640,61 @@
             arrived(W.at[i, pl.ds(core, 4)], out_recv.at[i]).wait()
         passes(k).start()
 
-    wide_lane = lax.broadcasted_iota(jnp.int32, (rows, lanes), 1)
-    source = (wide_lane - amount) & (lanes - 1)
-    inside = wide_lane >= amount
-
     def rotate(field):
-        chunks = [field[:, v * lanes : (v + 1) * lanes] for v in range(GROUPS)]
-        turned = [jnp.take_along_axis(chunk, source, axis=1) for chunk in chunks]
-        return jnp.concatenate(
-            [jnp.where(inside, turned[v], turned[v - 1]) for v in range(GROUPS)], axis=1
-        )
-
-    total = GROUPS * lanes
-    at = jnp.full((TILE, total), place, jnp.int32)
-    lowest = at == 0
-    highest = at == 2 * blocks * n_rad - 1
+        out = [[None] * GROUPS for _ in range(GROUPS)]
+        for w in range(GROUPS):
+            near_by = [jnp.where(odd[w], field[u - 1][w], field[u][w]) for u in range(GROUPS)]
+            for u in range(GROUPS):
+                chosen = jnp.where(two[w], near_by[u - 2], near_by[u])
+                out[u][w] = jnp.take_along_axis(chosen, source[u][w], axis=1)
+        return out
+
+    at = jnp.full((TILE, lanes), place, jnp.int32)
+    lowest = jnp.logical_and(at == 0, row < 2)
+    highest = jnp.logical_and(at == 2 * blocks * n_rad - 1, row >= TILE - 2)
 
     def edged(field):
-        low = jnp.broadcast_to(field[TILE : TILE + 1], (TILE, total))
-        high = jnp.broadcast_to(field[3 * TILE - 1 : 3 * TILE], (TILE, total))
-        return jnp.concatenate(
-            [
-                jnp.where(lowest, low, field[:TILE]),
-                field[TILE : 3 * TILE],
-                jnp.where(highest, high, field[3 * TILE :]),
-            ],
-            axis=0,
-        )
-
+        out = []
+        for u in range(GROUPS):
+            low = jnp.broadcast_to(field[u][0][2:3], (TILE, lanes))
+            high = jnp.broadcast_to(field[u][3][TILE - 3 : TILE - 2], (TILE, lanes))
+            out.append(
+                [jnp.where(highest, high, field[u][w]) for w in range(2)]
+                + [jnp.where(lowest, low, field[u][w]) for w in range(2, GROUPS)]
+            )
+        return out
+
+    def unpack(parts):
+        return [lane_rows(part, -TILE * g) for g, part in enumerate(exchange(parts, lane_of[parts[0].shape[0]]))]
+
+    lane_of = {n * TILE: lax.broadcasted_iota(jnp.int32, (n * TILE, lanes), 1) for n in (1, 2, 3)}
+
+    direct = unpack([W[i, 1:4].reshape(3 * TILE, lanes) for i in range(n_az)])
+    for g in range(GROUPS * GROUPS):
+        F[g, pl.ds(pl.multiple_of(core * TILE, TILE), 3 * TILE)] = direct[g]
+    for g, part in enumerate(unpack([W[i, 4 * core] for i in range(n_az)])):
+        w, u = g // GROUPS, g % GROUPS
+        F[GROUPS * GROUPS + u, w * TILE : (w + 1) * TILE] = part
     for q in range(GROUPS):
         passed(q).wait_recv()
-
-    columns = []
-    for v in range(GROUPS):
-        parts = [W[GROUPS * v + b, pl.ds(1 - core, 4)].reshape(rows, lanes) for b in range(GROUPS)]
-        columns.append(regroup(parts, wide_lane))
-    state = [edged(jnp.concatenate([columns[v][f] for v in range(GROUPS)], axis=1)) for f in range(4)]
+    for g, part in enumerate(unpack([W[i, 4 - 4 * core] for i in range(n_az)])):
+        F[g, pl.ds(pl.multiple_of((1 - core) * 3 * TILE, TILE), TILE)] = part
+
+    state = [
+        [[F[GROUPS * f + u, pl.ds(w, TILE, stride=GROUPS), :] for w in range(GROUPS)] for u in range(GROUPS)]
+        for f in range(fields)
+    ]
     step = advect_all(state)
     state = [edged(rotate(step(field))) for field in state]
-
-    columns = [regroup([W[GROUPS * v + b, 4 * core] for b in range(GROUPS)], lane) for v in range(GROUPS)]
-    field = jnp.concatenate(
-        [jnp.concatenate([columns[v][w] for v in range(GROUPS)], axis=1) for w in range(4)], axis=0
-    )
-    state.append(edged(rotate(step(edged(field)))))
-
     mr, mp, en = push_all(state)
     state = [edged(field) for field in (state[0], mr, mp, state[3], en)]
     step = advect_all(state)
+    state = [edged(rotate(step(field))) for field in state]
+    mr, mp, en = push_all(state)
+    for f, field in enumerate((state[0], mr, mp, state[3], en)):
+        for u in range(GROUPS):
+            for w in range(GROUPS):
+                G[GROUPS * f + u, pl.ds(w, TILE, stride=GROUPS), :] = field[u][w]
 
     order = [(k, j) for k in (2, 1, 3, 0) for j in [*range(1, plane), 0]]
 
@@ -623,32 +703,25 @@
         i = lax.rem(me // plane + k, GROUPS) * plane + lax.rem(me + j, plane)
         src, dst = B.at[i], R.at[layer, block, core]
         sems = back_send.at[index], back_recv.at[(layer * blocks + block) * 2 + core]
-        across = remote(src, dst, *sems, {"az": i, "rad": half})
-        return across, None if k or j else pltpu.make_async_copy(src, dst, sems[1])
-
-    def pack(to, fields2):
-        for v in range(GROUPS):
-            cut = slice(v * lanes, (v + 1) * lanes)
-            parts = [f[(1 + t) * TILE : (2 + t) * TILE, cut] for f in fields2 for t in range(2)]
-            for b, part in enumerate(regroup(parts, lane)):
-                B[GROUPS * v + b, to * TILE : (to + 1) * TILE] = part
-
-    rho, mz = (edged(rotate(step(state[f]))) for f in (0, 3))
-    pack(0, (rho, mz))
-    mr, mp, en = (edged(rotate(step(state[f]))) for f in (1, 2, 4))
-    mr, mp, en = push_all((rho, mr, mp, mz, en))
-    pack(1, (mr, mp))
-    for v in range(GROUPS // 2):
-        cuts = [slice(u * lanes, (u + 1) * lanes) for u in (v, v + GROUPS // 2)]
-        parts = [en[(1 + t) * TILE : (2 + t) * TILE, cut] for cut in cuts for t in range(2)]
-        for b, part in enumerate(regroup(parts, lane)):
-            folded = fold(part, lane, row)
-            B[GROUPS * v + b, 2 * TILE :] = folded[: TILE // 2]
-            B[GROUPS * (v + GROUPS // 2) + b, 2 * TILE :] = folded[TILE // 2 :]
+        sent = remote(src, dst, *sems, {"az": i, "rad": half})
+        return sent, None if k or j else pltpu.make_async_copy(src, dst, sems[1])
+
+    own = [lane_rows(G[g, TILE : 3 * TILE], TILE * g) for g in range(GROUPS * GROUPS)]
+    for i, part in enumerate(exchange(own, lane_of[2 * TILE])):
+        B[i, : 2 * TILE] = part
+    own = [
+        lane_rows(G[GROUPS * GROUPS + u, (1 + t) * TILE : (2 + t) * TILE], TILE * (GROUPS * t + u))
+        for t in range(2)
+        for u in range(GROUPS)
+    ]
+    for i, part in enumerate(exchange(own, lane)):
+        folded = fold(lane_rows(part, -TILE * i), lane, row)
+        B[i, 2 * TILE :] = folded[: TILE // 2]
+        B[i + n_az // 2, 2 * TILE :] = folded[TILE // 2 :]
     for index in range(len(order)):
-        across, within = back(index)
+        sent, within = back(index)
         if within is None:
-            across.start()
+            sent.start()
         else:
 
             @pl.when(here)
@@ -657,30 +730,19 @@
 
             @pl.when(jnp.logical_not(here))
             def _():
-                across.start()
+                sent.start()
 
     for l in range(depth):
         for s in range(blocks):
             for c in range(2):
                 arrived(R.at[l, s, c], back_recv.at[(l * blocks + s) * 2 + c]).wait()
     for l in range(depth):
-        pieces = []
-        for s in range(blocks):
-            for c in range(2):
-                first, second = R[l, s, c, :TILE], R[l, s, c, TILE : 2 * TILE]
-                for t in range(2):
-                    a = lane_rows(first, width if t == 0 else -width)
-                    b = lane_rows(second, width if t == 0 else -width)
-                    if t == 0:
-                        p, q, r, u = first, b, second, a
-                    else:
-                        p, q, r, u = a, second, b, first
-                    pieces.append(
-                        jnp.where(group < 2, jnp.where(group == 0, p, q), jnp.where(group == 2, r, u))
-                    )
-        block_out = jnp.concatenate(pieces, axis=0).T
-        for f in range(4):
-            out[f, l] = block_out[f * width : (f + 1) * width]
+        pieces = [R[l, s, c, : 2 * TILE] for s in range(blocks) for c in range(2)]
+        cells = pltpu.roll(jnp.concatenate(pieces, axis=0), lax.rem(lanes - spin, lanes), 1).T
+        for f in range(GROUPS):
+            for u in range(GROUPS):
+                g = GROUPS * f + u
+                out[f, l, pl.ds(u, TILE, stride=GROUPS), :] = cells[g * TILE : (g + 1) * TILE]
     pieces = []
     for s in range(blocks):
         both = [fold(jnp.concatenate([R[l, s, c, 2 * TILE :] for c in range(2)], axis=0), lane, row) for l in range(depth)]
@@ -689,35 +751,37 @@
             for l in range(1, depth):
                 piece = jnp.where(group == l, lane_rows(both[l], width * (l - g)), piece)
             pieces.append(piece)
-    block_out = jnp.concatenate(pieces, axis=0).T
+    cells = jnp.concatenate(pieces, axis=0).T
     for l in range(depth):
-        out[4, l] = block_out[l * width : (l + 1) * width]
+        for u in range(GROUPS):
+            g = GROUPS * l + u
+            out[4, l, pl.ds(u, TILE, stride=GROUPS), :] = cells[g * TILE : (g + 1) * TILE]
 
     swap_shift.wait_send()
     for l in range(depth):
         for copy in swaps(l, True):
             copy.wait_send()
     for index in range(len(targets)):
-        across, within, _ = send(index)
+        sent, within, _ = send(index)
         if within is None:
-            across.wait_send()
+            sent.wait_send()
         else:
 
             @pl.when(jnp.logical_not(here))
             def _():
-                across.wait_send()
+                sent.wait_send()
 
     for k in range(GROUPS):
         passes(k).wait_send()
     for index in range(len(order)):
-        across, within = back(index)
+        sent, within = back(index)
         if within is None:
-            across.wait_send()
+            sent.wait_send()
         else:
 
             @pl.when(jnp.logical_not(here))
             def _():
-                across.wait_send()
+                sent.wait_send()
 
 
 def turned_body(mesh, state, shifts):
@@ -741,6 +805,9 @@
             vmem(n_az, 5, *tile),
             pltpu.VMEM((1, lanes), jnp.int32),
             pltpu.VMEM((2 * lanes + 2 * TILE, lanes), jnp.int32),
+            pltpu.VMEM((4 * TILE, lanes), jnp.int32),
+            vmem(GROUPS * fields, 4 * TILE, lanes),
+            vmem(GROUPS * fields, 4 * TILE, lanes),
             vmem(n_az, 2 * TILE + TILE // 2, lanes),
             vmem(depth, blocks, 2, 2 * TILE + TILE // 2, lanes),
             dma((depth,)),
@@ -766,6 +833,8 @@
         and fields == GROUPS + 1
         and width * GROUPS == lanes
         and n_az == GROUPS * GROUPS
+        and width == GROUPS * TILE
+        and lanes == n_az * TILE
         and n_az % (depth * n_rad) == 0
         and tiles == GROUPS * (n_az // (depth * n_rad))
         and depth * width <= lanes

time: 27.6 us -> 24.7 us (0.89)
  Pallas kernels: 26.8 us -> 23.9 us
    pallas_call x1, Pallas kernels: 26.8 us -> 23.9 us  [turned_body(): pl.pallas_call(functools.partial(turned_kernel, n_az, n_rad), out_shape=p...]
where the time goes in v4:
time: 24.7 us; the launch traced here: 24.6 us
  Pallas kernels  23.9 us (97%)
  local copies, waits for them, and re-layouts  0.67 us (3%)
    pallas_call x1, Pallas kernels, turned_body(): pl.pallas_call(functools.partial(turned_kernel, n_az, n_rad), out_shape=p...  23.9 us
    unnamed x1, local copies, waits for them, and re-layouts  0.67 us

profile of v4, /device:TPU:0, one launch (start us, length us, event | category | flops | bytes accessed | tf_op | source)
XLA Modules:
  0.0 24.6 jit_solution(4803175450720552945)
XLA Ops:
  0.0 23.9 %shard_map.28 = f32[5,2,32,128]{3,2,1,0:T(8,128)S(1)} custom-call(f32[5,2,32,128]{3,2,1,0:T(8,128)} %x_in.1, s32[1,128]{1,0:T(1,128)} %bitcast.1), custom_call_target="tpu_custom_call" | custom-call | tf_op jit(solution)/shard_map/pallas_call | solution.py:795
  23.9 0.7 %copy.4 = f32[5,2,32,128]{3,2,1,0:T(8,128)} copy(f32[5,2,32,128]{3,2,1,0:T(8,128)S(1)} %shard_map.28) | data formatting | bytes 327680

commit v5 on v4

--- a/solution.py
+++ b/solution.py
@@ -519,15 +519,16 @@
         own = EP[l, 1 + s]
         if c == 0:
             M[l, s, c, 0] = pltpu.roll(jnp.where(group == GROUPS - 1, EP[l, s], own), lax.rem(spin + width, lanes), 1)
-            M[l, s, c, 1:4] = T4[l, GROUPS * s : GROUPS * s + 3]
+            M[l, s, c, 1:3] = T4[l, GROUPS * s : GROUPS * s + 2]
         else:
-            M[l, s, c, 0:3] = T4[l, GROUPS * s + 3 : GROUPS * s + 6]
+            M[l, s, c, 1:3] = T4[l, GROUPS * s + 4 : GROUPS * s + 6]
             M[l, s, c, 3] = pltpu.roll(jnp.where(group == 0, EP[l, s + 2], own), lax.rem(spin + lanes - width, lanes), 1)
 
     late = ((0, 0), (blocks - 1, 1))
     for l in range(depth):
         for s in range(blocks):
             for c in range(2):
+                M[l, s, c, 3 - 3 * c] = T4[l, GROUPS * s + 2 + c]
                 if (s, c) not in late:
                     stage(l, s, c)
 
@@ -559,45 +560,43 @@
 
     targets = [(ks, kl, kc) for ks in (2, 1, 3, 0) for kl in range(depth) for kc in (1, 0)]
 
-    def send(index):
+    def send(index, first):
         ks, kl, kc = targets[index]
         s = lax.rem(block + ks, blocks)
         l = lax.rem(layer + kl, depth)
         c = lax.rem(core + kc, 2)
-        src, dst = M.at[l, s, c], W.at[me, pl.ds(c, 4)]
-        sems = out_send.at[index], out_recv.at[me]
+        if first:
+            src, dst = M.at[l, s, c, 3 - 3 * c], W.at[me, 3 - 2 * c]
+            sems = out_send.at[0, index], out_recv.at[0, me]
+        else:
+            src, dst = M.at[l, s, c, pl.ds(c, 3)], W.at[me, pl.ds(2 * c, 3)]
+            sems = out_send.at[1, index], out_recv.at[1, me]
         sent = remote(src, dst, *sems, {"az": (s * depth + l) * n_rad + core, "rad": c})
         is_late = s == c * (blocks - 1)
         return sent, None if ks or kl or kc else pltpu.make_async_copy(src, dst, sems[1]), is_late
 
-    def start(want_late):
+    def start(first, when=None):
         for index in range(len(targets)):
-            sent, within, is_late = send(index)
-            now = is_late if want_late else jnp.logical_not(is_late)
-            if within is None:
-
-                @pl.when(now)
+            sent, within, is_late = send(index, first)
+            if within is None and when is None:
+                sent.start()
+                continue
+            now = True if when is None else when(is_late)
+            for copy, also in ((sent, None),) if within is None else ((within, here), (sent, jnp.logical_not(here))):
+
+                @pl.when(now if also is None else jnp.logical_and(now, also))
                 def _():
-                    sent.start()
-
-            else:
-
-                @pl.when(jnp.logical_and(now, here))
-                def _():
-                    within.start()
-
-                @pl.when(jnp.logical_and(now, jnp.logical_not(here)))
-                def _():
-                    sent.start()
-
-    start(False)
+                    copy.start()
+
+    start(True)
+    start(False, jnp.logical_not)
     for l in range(depth):
         for copy in swaps(l, True):
             copy.wait_recv()
     for l in range(depth):
         for s, c in late:
             stage(l, s, c)
-    start(True)
+    start(False, lambda is_late: is_late)
 
     swap_shift.wait_recv()
     lower = jnp.full((1, lanes), core, jnp.int32) == 0
@@ -637,7 +636,7 @@
     for k in range(GROUPS):
         for j in range(plane):
             i = near[k] * plane + lax.rem(me + j, plane)
-            arrived(W.at[i, pl.ds(core, 4)], out_recv.at[i]).wait()
+            arrived(W.at[i, 3 - 2 * core], out_recv.at[0, i]).wait()
         passes(k).start()
 
     def rotate(field):
@@ -669,6 +668,10 @@
 
     lane_of = {n * TILE: lax.broadcasted_iota(jnp.int32, (n * TILE, lanes), 1) for n in (1, 2, 3)}
 
+    for k in range(GROUPS):
+        for j in range(plane):
+            i = near[k] * plane + lax.rem(me + j, plane)
+            arrived(W.at[i, pl.ds(2 * core, 3)], out_recv.at[1, i]).wait()
     direct = unpack([W[i, 1:4].reshape(3 * TILE, lanes) for i in range(n_az)])
     for g in range(GROUPS * GROUPS):
         F[g, pl.ds(pl.multiple_of(core * TILE, TILE), 3 * TILE)] = direct[g]
@@ -761,15 +764,16 @@
     for l in range(depth):
         for copy in swaps(l, True):
             copy.wait_send()
-    for index in range(len(targets)):
-        sent, within, _ = send(index)
-        if within is None:
-            sent.wait_send()
-        else:
-
-            @pl.when(jnp.logical_not(here))
-            def _():
+    for first in (True, False):
+        for index in range(len(targets)):
+            sent, within, _ = send(index, first)
+            if within is None:
                 sent.wait_send()
+            else:
+
+                @pl.when(jnp.logical_not(here))
+                def _():
+                    sent.wait_send()
 
     for k in range(GROUPS):
         passes(k).wait_send()
@@ -813,8 +817,8 @@
             dma((depth,)),
             dma((2,)),
             dma((4, depth)),
-            dma((n_az,)),
-            dma((n_az,)),
+            dma((2, n_az)),
+            dma((2, n_az)),
             dma((GROUPS,)),
             dma((GROUPS,)),
             dma((n_az,)),

time: 24.7 us -> 24.2 us (0.980)
  Pallas kernels: 23.9 us -> 23.4 us
    pallas_call x1, Pallas kernels: 23.9 us -> 23.4 us  [turned_body(): pl.pallas_call(functools.partial(turned_kernel, n_az, n_rad), out_shape=p...]
where the time goes in v5:
time: 24.2 us; the launch traced here: 24.1 us
  Pallas kernels  23.4 us (97%)
  local copies, waits for them, and re-layouts  0.67 us (3%)
    pallas_call x1, Pallas kernels, turned_body(): pl.pallas_call(functools.partial(turned_kernel, n_az, n_rad), out_shape=p...  23.4 us
    unnamed x1, local copies, waits for them, and re-layouts  0.67 us

profile of v5, /device:TPU:0, one launch (start us, length us, event | category | flops | bytes accessed | tf_op | source)
XLA Modules:
  0.0 24.1 jit_solution(14087932852594197597)
XLA Ops:
  0.0 23.4 %shard_map.28 = f32[5,2,32,128]{3,2,1,0:T(8,128)S(1)} custom-call(f32[5,2,32,128]{3,2,1,0:T(8,128)} %x_in.1, s32[1,128]{1,0:T(1,128)} %bitcast.1), custom_call_target="tpu_custom_call" | custom-call | tf_op jit(solution)/shard_map/pallas_call | solution.py:799
  23.4 0.7 %copy.4 = f32[5,2,32,128]{3,2,1,0:T(8,128)} copy(f32[5,2,32,128]{3,2,1,0:T(8,128)S(1)} %shard_map.28) | data formatting | bytes 327680

commit v6 on v5

--- a/solution.py
+++ b/solution.py
@@ -703,11 +703,19 @@
 
     def back(index):
         k, j = order[index]
-        i = lax.rem(me // plane + k, GROUPS) * plane + lax.rem(me + j, plane)
+        n = order.index((k, j))
+        if n == 0:
+            i = 0
+        elif n < 4:
+            i = 1 + lax.rem(me + n - 1, 3)
+        elif n < 8:
+            i = 4 + lax.rem(me + n + 1, 4)
+        else:
+            i = 8 + lax.rem(me + n + 1, 8)
         src, dst = B.at[i], R.at[layer, block, core]
         sems = back_send.at[index], back_recv.at[(layer * blocks + block) * 2 + core]
         sent = remote(src, dst, *sems, {"az": i, "rad": half})
-        return sent, None if k or j else pltpu.make_async_copy(src, dst, sems[1])
+        return sent, None if n not in (0, 3, 7, 15) else pltpu.make_async_copy(src, dst, sems[1]), i == me
 
     own = [lane_rows(G[g, TILE : 3 * TILE], TILE * g) for g in range(GROUPS * GROUPS)]
     for i, part in enumerate(exchange(own, lane_of[2 * TILE])):
@@ -722,16 +730,16 @@
         B[i, 2 * TILE :] = folded[: TILE // 2]
         B[i + n_az // 2, 2 * TILE :] = folded[TILE // 2 :]
     for index in range(len(order)):
-        sent, within = back(index)
+        sent, within, same = back(index)
         if within is None:
             sent.start()
         else:
 
-            @pl.when(here)
+            @pl.when(jnp.logical_and(here, same))
             def _():
                 within.start()
 
-            @pl.when(jnp.logical_not(here))
+            @pl.when(jnp.logical_not(jnp.logical_and(here, same)))
             def _():
                 sent.start()
 
@@ -778,12 +786,12 @@
     for k in range(GROUPS):
         passes(k).wait_send()
     for index in range(len(order)):
-        sent, within = back(index)
+        sent, within, same = back(index)
         if within is None:
             sent.wait_send()
         else:
 
-            @pl.when(jnp.logical_not(here))
+            @pl.when(jnp.logical_not(jnp.logical_and(here, same)))
             def _():
                 sent.wait_send()
 

time: 24.2 us -> 23.2 us (0.959)
  Pallas kernels: 23.4 us -> 22.3 us
    pallas_call x1, Pallas kernels: 23.4 us -> 22.3 us  [turned_body(): pl.pallas_call(functools.partial(turned_kernel, n_az, n_rad), out_shape=p...]
where the time goes in v6:
time: 23.2 us; the launch traced here: 23 us
  Pallas kernels  22.3 us (96%)
  local copies, waits for them, and re-layouts  0.67 us (3%)
    pallas_call x1, Pallas kernels, turned_body(): pl.pallas_call(functools.partial(turned_kernel, n_az, n_rad), out_shape=p...  22.3 us
    unnamed x1, local copies, waits for them, and re-layouts  0.67 us

profile of v6, /device:TPU:0, one launch (start us, length us, event | category | flops | bytes accessed | tf_op | source)
XLA Modules:
  0.0 23.0 jit_solution(10962147242152950861)
XLA Ops:
  0.0 22.3 %shard_map.28 = f32[5,2,32,128]{3,2,1,0:T(8,128)S(1)} custom-call(f32[5,2,32,128]{3,2,1,0:T(8,128)} %x_in.1, s32[1,128]{1,0:T(1,128)} %bitcast.1), custom_call_target="tpu_custom_call" | custom-call | tf_op jit(solution)/shard_map/pallas_call | solution.py:807
  22.3 0.7 %copy.4 = f32[5,2,32,128]{3,2,1,0:T(8,128)} copy(f32[5,2,32,128]{3,2,1,0:T(8,128)S(1)} %shard_map.28) | data formatting | bytes 327680

commit v7 on v6

--- a/solution.py
+++ b/solution.py
@@ -399,12 +399,11 @@
     return flux - last_of(flux, axis)
 
 
-def line_push(pressure, density, speed, axis, courant):
+def line_push(pressure, density, speed, axis):
     compress = jnp.minimum(next_of(speed, axis) - last_of(speed, axis), 0.0)
-    total = pressure + VISCOSITY_COEF * density * compress * compress
+    total = pressure + density * compress * compress
     work = total * speed
-    scale = -0.5 * courant
-    return scale * (next_of(total, axis) - last_of(total, axis)), scale * (next_of(work, axis) - last_of(work, axis))
+    return next_of(total, axis) - last_of(total, axis), next_of(work, axis) - last_of(work, axis)
 
 
 def advect_all(state):
@@ -428,22 +427,26 @@
 
 
 def push_all(state):
+    scale = -0.5 * COURANT_AZIMUTH
+    assert COURANT_RADIAL == COURANT_AZIMUTH
     rho, mr, mp, mz, energy = state
-    inverse, pressure, new_mr, rest = [], [], [], []
+    inverse, pressure, density, new_mr, rest = [], [], [], [], []
     for u in range(GROUPS):
         r, a, b, c, e = (across(f, u) for f in state)
         inv = 1.0 / r
-        p = (GAMMA_GAS - 1.0) * (e - 0.5 * (a * a + b * b + c * c) * inv)
-        rad_m, rad_e = line_push(p, r, a * inv, 0, COURANT_RADIAL)
+        p = (scale * (GAMMA_GAS - 1.0)) * (e - 0.5 * (a * a + b * b + c * c) * inv)
+        d = (scale * VISCOSITY_COEF) * r
+        rad_m, rad_e = line_push(p, d, a * inv, 0)
         inverse.append(tiles_of(inv))
         pressure.append(tiles_of(p))
+        density.append(tiles_of(d))
         new_mr.append(tiles_of(a + rad_m))
         rest.append(tiles_of(e + rad_e))
     new_mp = [[None] * GROUPS for _ in range(GROUPS)]
     new_energy = [[None] * GROUPS for _ in range(GROUPS)]
     for w in range(GROUPS):
         b = along(mp, w)
-        az_m, az_e = line_push(along(pressure, w), along(rho, w), b * along(inverse, w), 1, COURANT_AZIMUTH)
+        az_m, az_e = line_push(along(pressure, w), along(density, w), b * along(inverse, w), 1)
         for u, (m, e) in enumerate(zip(tiles_of(b + az_m), tiles_of(along(rest, w) + az_e))):
             new_mp[u][w], new_energy[u][w] = m, e
     return new_mr, new_mp, new_energy
@@ -459,9 +462,9 @@
     MESH = pl.DeviceIdType.MESH
     me = lax.axis_index("az")
     core = lax.axis_index("rad")
-    half = lax.rem(me, n_rad)
-    layer = lax.rem(me // n_rad, depth)
-    block = me // (n_rad * depth)
+    half = lax.rem(me // 2, 2)
+    layer = lax.rem(me, 2)
+    block = me // 4
     place = (half * blocks + block) * 2 + core
     partner = {"rad": 1 - core}
     here = half == core
@@ -558,7 +561,9 @@
             for copy in swaps(l, False):
                 copy.start()
 
-    targets = [(ks, kl, kc) for ks in (2, 1, 3, 0) for kl in range(depth) for kc in (1, 0)]
+    whole = ()
+    split = (2, 1, 3, 0)
+    targets = [(ks, kl, kc) for ks in (*whole, *split) for kl in (1, 0) for kc in (0, 1)]
 
     def send(index, first):
         ks, kl, kc = targets[index]
@@ -569,14 +574,22 @@
             src, dst = M.at[l, s, c, 3 - 3 * c], W.at[me, 3 - 2 * c]
             sems = out_send.at[0, index], out_recv.at[0, me]
         else:
-            src, dst = M.at[l, s, c, pl.ds(c, 3)], W.at[me, pl.ds(2 * c, 3)]
+            if ks in split:
+                src, dst = M.at[l, s, c, pl.ds(c, 3)], W.at[me, pl.ds(2 * c, 3)]
+            else:
+                src, dst = M.at[l, s, c], W.at[me, pl.ds(c, 4)]
             sems = out_send.at[1, index], out_recv.at[1, me]
-        sent = remote(src, dst, *sems, {"az": (s * depth + l) * n_rad + core, "rad": c})
+        sent = remote(src, dst, *sems, {"az": s * 4 + core * 2 + l, "rad": c})
         is_late = s == c * (blocks - 1)
         return sent, None if ks or kl or kc else pltpu.make_async_copy(src, dst, sems[1]), is_late
 
+    messages = [(index, True) for index, t in enumerate(targets) if t[0] in split]
+    messages += [(index, False) for index in range(len(targets))]
+
     def start(first, when=None):
-        for index in range(len(targets)):
+        for index, part in messages:
+            if part != first:
+                continue
             sent, within, is_late = send(index, first)
             if within is None and when is None:
                 sent.start()
@@ -618,11 +631,15 @@
     ]
 
     plane = n_az // GROUPS
-    near = [lax.rem(me // plane + k, GROUPS) for k in (0, 1, 3, 2)]
-
-    def passes(k):
-        ahead = pl.ds(near[k] * plane, plane)
-        return remote(W.at[ahead, 3 - 2 * core], W.at[ahead, 4 * core], pass_send.at[k], pass_recv.at[near[k]], partner)
+
+    def sender(ks):
+        return lax.rem(block + blocks - ks, blocks)
+
+    def passes(ks):
+        ahead = pl.ds(sender(ks) * plane, plane)
+        return remote(
+            W.at[ahead, 3 - 2 * core], W.at[ahead, 4 * core], pass_send.at[ks], pass_recv.at[sender(ks)], partner
+        )
 
     def passed(q):
         return remote(
@@ -633,11 +650,22 @@
     def arrived(dst, recv):
         return pltpu.make_async_copy(dst, dst, recv)
 
-    for k in range(GROUPS):
+    def await_senders(ks, first):
         for j in range(plane):
-            i = near[k] * plane + lax.rem(me + j, plane)
-            arrived(W.at[i, 3 - 2 * core], out_recv.at[0, i]).wait()
-        passes(k).start()
+            i = sender(ks) * plane + lax.rem(me + j, plane)
+            if first:
+                arrived(W.at[i, 3 - 2 * core], out_recv.at[0, i]).wait()
+            elif ks in split:
+                arrived(W.at[i, pl.ds(2 * core, 3)], out_recv.at[1, i]).wait()
+            else:
+                arrived(W.at[i, pl.ds(core, 4)], out_recv.at[1, i]).wait()
+
+    for ks in split:
+        await_senders(ks, True)
+        passes(ks).start()
+    for ks in whole:
+        await_senders(ks, False)
+        passes(ks).start()
 
     def rotate(field):
         out = [[None] * GROUPS for _ in range(GROUPS)]
@@ -668,20 +696,19 @@
 
     lane_of = {n * TILE: lax.broadcasted_iota(jnp.int32, (n * TILE, lanes), 1) for n in (1, 2, 3)}
 
-    for k in range(GROUPS):
-        for j in range(plane):
-            i = near[k] * plane + lax.rem(me + j, plane)
-            arrived(W.at[i, pl.ds(2 * core, 3)], out_recv.at[1, i]).wait()
-    direct = unpack([W[i, 1:4].reshape(3 * TILE, lanes) for i in range(n_az)])
-    for g in range(GROUPS * GROUPS):
-        F[g, pl.ds(pl.multiple_of(core * TILE, TILE), 3 * TILE)] = direct[g]
+    def settle(slot, at_row):
+        for g, part in enumerate(unpack([W[i, pl.ds(slot, 2)].reshape(2 * TILE, lanes) for i in range(n_az)])):
+            F[g, pl.ds(pl.multiple_of(at_row, TILE), 2 * TILE)] = part
+
+    for q in range(GROUPS):
+        passed(q).wait_recv()
+    settle(3 - 3 * core, 2 * TILE * (1 - core))
+    for ks in split:
+        await_senders(ks, False)
+    settle(1 + core, 2 * TILE * core)
     for g, part in enumerate(unpack([W[i, 4 * core] for i in range(n_az)])):
         w, u = g // GROUPS, g % GROUPS
         F[GROUPS * GROUPS + u, w * TILE : (w + 1) * TILE] = part
-    for q in range(GROUPS):
-        passed(q).wait_recv()
-    for g, part in enumerate(unpack([W[i, 4 - 4 * core] for i in range(n_az)])):
-        F[g, pl.ds(pl.multiple_of((1 - core) * 3 * TILE, TILE), TILE)] = part
 
     state = [
         [[F[GROUPS * f + u, pl.ds(w, TILE, stride=GROUPS), :] for w in range(GROUPS)] for u in range(GROUPS)]
@@ -747,7 +774,6 @@
         for s in range(blocks):
             for c in range(2):
                 arrived(R.at[l, s, c], back_recv.at[(l * blocks + s) * 2 + c]).wait()
-    for l in range(depth):
         pieces = [R[l, s, c, : 2 * TILE] for s in range(blocks) for c in range(2)]
         cells = pltpu.roll(jnp.concatenate(pieces, axis=0), lax.rem(lanes - spin, lanes), 1).T
         for f in range(GROUPS):
@@ -772,16 +798,15 @@
     for l in range(depth):
         for copy in swaps(l, True):
             copy.wait_send()
-    for first in (True, False):
-        for index in range(len(targets)):
-            sent, within, _ = send(index, first)
-            if within is None:
+    for index, first in messages:
+        sent, within, _ = send(index, first)
+        if within is None:
+            sent.wait_send()
+        else:
+
+            @pl.when(jnp.logical_not(here))
+            def _():
                 sent.wait_send()
-            else:
-
-                @pl.when(jnp.logical_not(here))
-                def _():
-                    sent.wait_send()
 
     for k in range(GROUPS):
         passes(k).wait_send()

time: 23.2 us -> 22.9 us (0.987)
  Pallas kernels: 22.3 us -> 22 us
    pallas_call x1, Pallas kernels: 22.3 us -> 22 us  [turned_body(): pl.pallas_call(functools.partial(turned_kernel, n_az, n_rad), out_shape=p...]
where the time goes in v7:
time: 22.9 us; the launch traced here: 22.7 us
  Pallas kernels  22 us (96%)
  local copies, waits for them, and re-layouts  0.67 us (3%)
    pallas_call x1, Pallas kernels, turned_body(): pl.pallas_call(functools.partial(turned_kernel, n_az, n_rad), out_shape=p...  22 us
    unnamed x1, local copies, waits for them, and re-layouts  0.67 us

profile of v7, /device:TPU:0, one launch (start us, length us, event | category | flops | bytes accessed | tf_op | source)
XLA Modules:
  0.0 22.7 jit_solution(7959911425805398156)
XLA Ops:
  0.0 22.0 %shard_map.28 = f32[5,2,32,128]{3,2,1,0:T(8,128)S(1)} custom-call(f32[5,2,32,128]{3,2,1,0:T(8,128)} %x_in.1, s32[1,128]{1,0:T(1,128)} %bitcast.1), custom_call_target="tpu_custom_call" | custom-call | tf_op jit(solution)/shard_map/pallas_call | solution.py:832
  22.0 0.7 %copy.4 = f32[5,2,32,128]{3,2,1,0:T(8,128)} copy(f32[5,2,32,128]{3,2,1,0:T(8,128)S(1)} %shard_map.28) | data formatting | bytes 327680

commit v8 on v7

--- a/solution.py
+++ b/solution.py
@@ -452,8 +452,8 @@
     return new_mr, new_mp, new_energy
 
 
-def turned_kernel(n_az, n_rad, x_in, shifts, out, *scratch):
-    (x, T4, EP, M, W, other, SC, AM, F, G, B, R, load_sem, shift_sem, swap_sem, out_send, out_recv, pass_send, pass_recv,
+def turned_kernel(n_az, n_rad, x_in, shifts_in, out, *scratch):
+    (x, T4, EP, M, W, shifts, other, SC, AM, F, G, B, R, load_sem, table_sem, shift_sem, swap_sem, out_send, out_recv, pass_send, pass_recv,
      back_send, back_recv) = scratch
     fields, depth, width, lanes = x.shape
     blocks = n_az // (depth * n_rad)
@@ -477,10 +477,12 @@
     loads = [pltpu.make_async_copy(x_in.at[:, l], x.at[:, l], load_sem.at[l]) for l in range(depth)]
     for load in loads:
         load.start()
+    table = pltpu.make_async_copy(shifts_in, shifts, table_sem)
+    table.start()
     barrier = pltpu.get_barrier_semaphore()
-    for k in range(1, n_az):
+    for k in range(n_az - 1):
         pl.semaphore_signal(
-            barrier, inc=1, device_id={"az": lax.rem(me + k, n_az), "rad": half}, device_id_type=MESH
+            barrier, inc=1, device_id={"az": k + (me <= k).astype(jnp.int32), "rad": half}, device_id_type=MESH
         )
     pl.semaphore_signal(barrier, inc=1, device_id=partner, device_id_type=MESH)
 
@@ -535,6 +537,475 @@
                 if (s, c) not in late:
                     stage(l, s, c)
 
+    table.wait()
+    senders = jnp.where(here, 2 * (n_az // n_rad - 1) + 1, 2 * (n_az // n_rad) + 1)
+    pl.semaphore_wait(barrier, senders)
+
+    whole = behind // width
+    tail = behind % width
+    tail_rows = -(-tail // TILE) * TILE
+    group = whole + 1
+    base = group * width
+    first_row = width - tail_rows
+    me = lax.axis_index("az")
+    place = lax.rem(me, group)
+    position = lax.axis_index("rad")
+
+    def az(by):
+        return {"az": lax.rem(me + by + n_az, n_az)}
+
+    def member(by):
+        return {"az": me - place + lax.rem(place + by + group, group)}
+
+    def rad(by):
+        return {"rad": position + by}
+
+    barrier = pltpu.get_barrier_semaphore()
+    MESH = pl.DeviceIdType.MESH
+    load = pltpu.make_async_copy(x_in, x, load_sem)
+    load.start()
+    for by in (1, -1, -group):
+        pl.semaphore_signal(barrier, inc=1, device_id=az(by), device_id_type=MESH)
+    for h in range(1, group):
+        pl.semaphore_signal(barrier, inc=1, device_id=member(h), device_id_type=MESH)
+
+    has_left = position > 0
+    has_right = position < n_rad - 1
+
+    @pl.when(has_left)
+    def _():
+        pl.semaphore_signal(barrier, inc=1, device_id=rad(-1), device_id_type=MESH)
+
+    @pl.when(has_right)
+    def _():
+        pl.semaphore_signal(barrier, inc=1, device_id=rad(1), device_id_type=MESH)
+
+    load.wait()
+    A[:, :, TILE : TILE + width, :] = x[...]
+    beside_me = (position + n_rad - 1) // n_rad + (2 * n_rad - 2 - position) // n_rad
+    pl.semaphore_wait(barrier, group + 2 + beside_me)
+
+    def remote(src, dst, send, recv, where):
+        return pltpu.make_async_remote_copy(
+            src_ref=src, dst_ref=dst, send_sem=send, recv_sem=recv, device_id=where, device_id_type=MESH
+        )
+
+    def ring_copies(z):
+        return [
+            remote(x.at[:, z, width - TILE : width], A.at[:, z, 0:TILE],
+                   state_send.at[0, z], state_recv.at[0, z], az(1)),
+            remote(x.at[:, z, 0:TILE], A.at[:, z, TILE + width : 2 * TILE + width],
+                   state_send.at[1, z], state_recv.at[1, z], az(-1)),
+        ]
+
+    def side_copies(phase, src, left_dst, right_dst, z):
+        to_right = remote(src.at[:, z], left_dst.at[:, z], side_send.at[phase, 0, z],
+                          side_recv.at[phase, 0, z], rad(1))
+        to_left = remote(src.at[:, z], right_dst.at[:, z], side_send.at[phase, 1, z],
+                         side_recv.at[phase, 1, z], rad(-1))
+        return to_right, to_left
+
+    def start_side(*args):
+        to_right, to_left = side_copies(*args)
+
+        @pl.when(has_right)
+        def _():
+            to_right.start()
+
+        @pl.when(has_left)
+        def _():
+            to_left.start()
+
+    def await_side(*args):
+        to_right, to_left = side_copies(*args)
+
+        @pl.when(has_left)
+        def _():
+            to_right.wait_recv()
+
+        @pl.when(has_right)
+        def _():
+            to_left.wait_recv()
+
+    def end_side(*args):
+        to_right, to_left = side_copies(*args)
+
+        @pl.when(has_right)
+        def _():
+            to_right.wait_send()
+
+        @pl.when(has_left)
+        def _():
+            to_left.wait_send()
+
+    windows = (W0, W1)
+    rotated = (O0, O1)
+    sides = ((x, L0, R0), (O0, L1, R1), (O1, L2, R2))
+
+    def gather_copies(step, f, z):
+        W = windows[step]
+        own, back = W.at[f, z, base : base + width], W.at[f, z, 0:width]
+        sems = lambda h: (gather_send.at[step, h, f, z], gather_recv.at[step, h, f, z])
+        onward = remote(own, back, *sems(0), az(group))
+        inside = []
+        for h in range(1, group):
+            dst = W.at[f, z, base - h * width : base - (h - 1) * width]
+            inside.append([remote(src, dst, *sems(h), member(h)) for src in (own, back)])
+        return onward, inside
+
+    def send_own(step, f, z):
+        onward, inside = gather_copies(step, f, z)
+        onward.start()
+        for h in range(1, group):
+
+            @pl.when(place + h < group)
+            def _():
+                inside[h - 1][0].start()
+
+    def pass_on(step, f, z):
+        onward, inside = gather_copies(step, f, z)
+        onward.wait_recv()
+        for h in range(1, group):
+
+            @pl.when(place + h >= group)
+            def _():
+                inside[h - 1][1].start()
+
+    def edges(own, left, right):
+        rows = own.shape[0]
+        lane = lax.broadcasted_iota(jnp.int32, (rows, lanes), 1)
+        at = jnp.full((rows, lanes), position, jnp.int32)
+        left = jnp.where(at == 0, jnp.broadcast_to(own[:, 0:1], own.shape), left)
+        right = jnp.where(at == n_rad - 1, jnp.broadcast_to(own[:, lanes - 1 : lanes], own.shape), right)
+        return jnp.where(lane < lanes // 2, right, left)
+
+    def wide(own, beside):
+        return jnp.concatenate([own, beside], axis=1)
+
+    def hydro(step, z, strip, beside):
+        rows = slice(TILE, TILE + width)
+        tall = [strip(f) for f in range(fields)]
+        az_speeds = face_speeds(tall[2] / tall[0], 0, COURANT_AZIMUTH)
+        broad = [wide(tall[f][rows], beside(f, tall[f][rows])) for f in range(fields)]
+        rad_speeds = face_speeds(broad[1] / broad[0], 1, COURANT_RADIAL)
+        for f in range(fields):
+            along = advect(tall[f], az_speeds, 0)[rows]
+            across = advect(broad[f], rad_speeds, 1)[:, :lanes]
+            windows[step][f, z, base : base + width, :] = tall[f][rows] - along - across
+            send_own(step, f, z)
+
+    def viscous(z, state, extended):
+        rho, mr, mp, mz, energy = state
+        own = slice(None) if extended else slice(0, lanes)
+        inverse = 1.0 / rho
+        pressure = (GAMMA_GAS - 1.0) * (energy - 0.5 * (mr * mr + mp * mp + mz * mz) * inverse)
+        az_m, az_e = push(pressure[:, own], rho[:, own], (mp * inverse)[:, own], 0, COURANT_AZIMUTH)
+        rad_m, rad_e = push(pressure, rho, mr * inverse, 1, COURANT_RADIAL)
+        return [
+            rho[:, own],
+            mr[:, own] + rad_m[:, own],
+            mp[:, own] + az_m,
+            mz[:, own],
+            energy[:, own] + az_e + rad_e[:, own],
+        ]
+
+    count = width + 2 * EDGE
+
+    for z in range(depth):
+        for copy in ring_copies(z):
+            copy.start()
+    for z in range(depth):
+        start_side(0, *sides[0], z)
+    for z in range(depth):
+        for copy in ring_copies(z):
+            copy.wait_recv()
+        await_side(0, *sides[0], z)
+        hydro(0, z, lambda f: A[f, z], lambda f, own: edges(own, L0[f, z], R0[f, z]))
+
+    for step in range(STEPS):
+        for z in range(depth):
+            for f in range(fields):
+                pass_on(step, f, z)
+        O, L, R = sides[step + 1]
+        for z in range(depth):
+            for f in range(fields):
+                for copies in gather_copies(step, f, z)[1]:
+                    copies[0].wait_recv()
+                start = base - first_row - EDGE
+                O[f, z] = shifted(windows[step][f, z, first_row:], start - shifts[...], count, start - SMIN)
+            start_side(step + 1, O, L, R, z)
+        for z in range(depth):
+            await_side(step + 1, O, L, R, z)
+            state = [wide(O[f, z], edges(O[f, z], L[f, z], R[f, z])) for f in range(fields)]
+            if step == STEPS - 1:
+                new = viscous(z, state, False)
+                for f in range(fields):
+                    out[f, z] = new[f][EDGE : EDGE + width]
+            else:
+                new = viscous(z, state, True)
+                A_rows = slice(TILE - EDGE, TILE - EDGE + count)
+                for f in range(fields):
+                    A[f, z, A_rows, :] = new[f][:, :lanes]
+                hydro(
+                    step + 1,
+                    z,
+                    lambda f: A[f, z],
+                    lambda f, own: edges(own, *[new[f][EDGE : EDGE + width, lanes:]] * 2),
+                )
+
+    for z in range(depth):
+        for copy in ring_copies(z):
+            copy.wait_send()
+        for phase in range(STEPS + 1):
+            end_side(phase, *sides[phase], z)
+        for step in range(STEPS):
+            for f in range(fields):
+                onward, inside = gather_copies(step, f, z)
+                onward.wait_send()
+                for copies in inside:
+                    copies[0].wait_send()
+
+
+def body(mesh, state, shifts):
+    n_az, n_rad = mesh.shape["az"], mesh.shape["rad"]
+    fields, depth, width, lanes = state.shape
+    behind = SMAX + EDGE
+    group = behind // width + 1
+    window = (group + 1) * width
+    count = width + 2 * EDGE
+    vmem = lambda rows: pltpu.VMEM((fields, depth, rows, lanes), jnp.float32)
+    dma = pltpu.SemaphoreType.DMA
+    return pl.pallas_call(
+        functools.partial(kernel, n_az, n_rad),
+        out_shape=pltpu.VMEM(state.shape, state.dtype),
+        in_specs=[pl.BlockSpec(memory_space=pl.ANY), pl.BlockSpec(memory_space=pltpu.VMEM)],
+        out_specs=pl.BlockSpec(memory_space=pltpu.VMEM),
+        scratch_shapes=[
+            vmem(width),
+            dma(()),
+            vmem(width + 2 * TILE),
+            vmem(window),
+            vmem(window),
+            vmem(count),
+            vmem(count),
+            vmem(width),
+            vmem(width),
+            vmem(count),
+            vmem(count),
+            vmem(count),
+            vmem(count),
+            dma((2, depth)),
+            dma((2, depth)),
+            dma((STEPS, group, fields, depth)),
+            dma((STEPS, group, fields, depth)),
+            dma((STEPS + 1, 2, depth)),
+            dma((STEPS + 1, 2, depth)),
+        ],
+        compiler_params=pltpu.CompilerParams(collective_id=0, has_side_effects=True),
+    )(state, shifts.reshape(1, -1))
+
+
+GROUPS = 4
+
+
+def lane_rows(x, shift):
+    return pltpu.roll(x, shift % x.shape[1], 1)
+
+
+def exchange(parts, lane):
+    n = len(parts)
+    out = [parts[-g % n] for g in range(n)]
+    for bit in range(n.bit_length() - 1):
+        far = (lane & (TILE << bit)) != 0
+        out = [jnp.where(far, out[(g - (1 << bit)) % n], out[g]) for g in range(n)]
+    return out
+
+
+def fold(x, lane, row):
+    half = x.shape[1] // 2
+    stay = (lane < half) == (row < TILE // 2)
+    return jnp.where(stay, x, lane_rows(pltpu.roll(x, TILE // 2, 0), half))
+
+
+def line(tiles):
+    return jnp.concatenate(tiles, axis=0)
+
+
+def tiles_of(x):
+    return [x[g * TILE : (g + 1) * TILE] for g in range(GROUPS)]
+
+
+def next_of(x, axis):
+    first = x[:TILE]
+    return jnp.concatenate([x[TILE:], pltpu.roll(first, first.shape[axis] - 1, axis)], axis=0)
+
+
+def last_of(x, axis):
+    last = x[-TILE:]
+    return jnp.concatenate([pltpu.roll(last, 1, axis), x[:-TILE]], axis=0)
+
+
+def along(field, w):
+    return line([field[u][w] for u in range(GROUPS)])
+
+
+def across(field, u):
+    return line(field[u])
+
+
+def line_speeds(velocity, axis, courant):
+    face = (0.5 * courant) * (velocity + next_of(velocity, axis))
+    return jnp.maximum(face, 0.0), jnp.minimum(face, 0.0)
+
+
+def line_advect(field, speeds, axis):
+    low = field - last_of(field, axis)
+    high = next_of(low, axis)
+    product = low * high
+    half = jnp.where(product > 0, product / (low + high), 0.0)
+    flux = speeds[0] * (field + half) + speeds[1] * next_of(field - half, axis)
+    return flux - last_of(flux, axis)
+
+
+def line_push(pressure, density, speed, axis):
+    compress = jnp.minimum(next_of(speed, axis) - last_of(speed, axis), 0.0)
+    total = pressure + density * compress * compress
+    work = total * speed
+    return next_of(total, axis) - last_of(total, axis), next_of(work, axis) - last_of(work, axis)
+
+
+def advect_all(state):
+    rho, mr, mp = state[:3]
+    az_speeds, rad_speeds = [], []
+    inverse = [tiles_of(1.0 / across(rho, u)) for u in range(GROUPS)]
+    for g in range(GROUPS):
+        az_speeds.append(line_speeds(along(mp, g) * along(inverse, g), 1, COURANT_AZIMUTH))
+        rad_speeds.append(line_speeds(across(mr, g) * across(inverse, g), 0, COURANT_RADIAL))
+
+    def step(field):
+        turned = [along(field, w) for w in range(GROUPS)]
+        turned = [tiles_of(turned[w] - line_advect(turned[w], az_speeds[w], 1)) for w in range(GROUPS)]
+        out = []
+        for u in range(GROUPS):
+            rest = line([turned[w][u] for w in range(GROUPS)])
+            out.append(tiles_of(rest - line_advect(across(field, u), rad_speeds[u], 0)))
+        return out
+
+    return step
+
+
+def push_all(state):
+    scale = -0.5 * COURANT_AZIMUTH
+    assert COURANT_RADIAL == COURANT_AZIMUTH
+    rho, mr, mp, mz, energy = state
+    inverse, pressure, density, new_mr, rest = [], [], [], [], []
+    for u in range(GROUPS):
+        r, a, b, c, e = (across(f, u) for f in state)
+        inv = 1.0 / r
+        p = (scale * (GAMMA_GAS - 1.0)) * (e - 0.5 * (a * a + b * b + c * c) * inv)
+        d = (scale * VISCOSITY_COEF) * r
+        rad_m, rad_e = line_push(p, d, a * inv, 0)
+        inverse.append(tiles_of(inv))
+        pressure.append(tiles_of(p))
+        density.append(tiles_of(d))
+        new_mr.append(tiles_of(a + rad_m))
+        rest.append(tiles_of(e + rad_e))
+    new_mp = [[None] * GROUPS for _ in range(GROUPS)]
+    new_energy = [[None] * GROUPS for _ in range(GROUPS)]
+    for w in range(GROUPS):
+        b = along(mp, w)
+        az_m, az_e = line_push(along(pressure, w), along(density, w), b * along(inverse, w), 1)
+        for u, (m, e) in enumerate(zip(tiles_of(b + az_m), tiles_of(along(rest, w) + az_e))):
+            new_mp[u][w], new_energy[u][w] = m, e
+    return new_mr, new_mp, new_energy
+
+
+def turned_kernel(n_az, n_rad, x_in, shifts_in, out, *scratch):
+    (x, T4, EP, M, W, shifts, other, SC, AM, F, G, B, R, load_sem, table_sem, shift_sem, swap_sem, out_send, out_recv, pass_send, pass_recv,
+     back_send, back_recv) = scratch
+    fields, depth, width, lanes = x.shape
+    blocks = n_az // (depth * n_rad)
+    tiles = lanes // TILE
+    rows = 4 * TILE
+    MESH = pl.DeviceIdType.MESH
+    me = lax.axis_index("az")
+    core = lax.axis_index("rad")
+    half = lax.rem(me // 2, 2)
+    layer = lax.rem(me, 2)
+    block = me // 4
+    place = (half * blocks + block) * 2 + core
+    partner = {"rad": 1 - core}
+    here = half == core
+
+    def remote(src, dst, send, recv, where):
+        return pltpu.make_async_remote_copy(
+            src_ref=src, dst_ref=dst, send_sem=send, recv_sem=recv, device_id=where, device_id_type=MESH
+        )
+
+    loads = [pltpu.make_async_copy(x_in.at[:, l], x.at[:, l], load_sem.at[l]) for l in range(depth)]
+    for load in loads:
+        load.start()
+    table = pltpu.make_async_copy(shifts_in, shifts, table_sem)
+    table.start()
+    barrier = pltpu.get_barrier_semaphore()
+    for k in range(n_az - 1):
+        pl.semaphore_signal(
+            barrier, inc=1, device_id={"az": k + (me <= k).astype(jnp.int32), "rad": half}, device_id_type=MESH
+        )
+    pl.semaphore_signal(barrier, inc=1, device_id=partner, device_id_type=MESH)
+
+    lane = lax.broadcasted_iota(jnp.int32, (TILE, lanes), 1)
+    row = lax.broadcasted_iota(jnp.int32, (TILE, lanes), 0)
+    group = lane // width
+
+    spin = me * TILE
+
+    def rows_of(f, l):
+        return [x[f, l, pl.ds(u, width // GROUPS, stride=GROUPS), :] for u in range(GROUPS)]
+
+    for l in range(depth):
+        loads[l].wait()
+        cells = jnp.concatenate([part for f in range(GROUPS) for part in rows_of(f, l)], axis=0)
+        T4[l, 1 : tiles + 1] = pltpu.roll(cells.T, spin, 1).reshape(tiles, TILE, lanes)
+    energy = [part for l in range(depth) for part in rows_of(4, l)]
+    turned = jnp.concatenate(energy * (lanes // (depth * width)), axis=0).T.reshape(tiles, TILE, lanes)
+    for l in range(depth):
+        for m in range(tiles // GROUPS):
+            packed = turned[GROUPS * m] if l == 0 else lane_rows(turned[GROUPS * m], -width * l)
+            for g in range(1, GROUPS):
+                packed = jnp.where(group == g, lane_rows(turned[GROUPS * m + g], width * (g - l)), packed)
+            EP[l, 1 + m] = packed
+
+    @pl.when(core == 0)
+    def _():
+        for l in range(depth):
+            T4[l, 0] = jnp.broadcast_to(T4[l, 1, 0:1], (TILE, lanes))
+            EP[l, 0] = jnp.broadcast_to(lane_rows(EP[l, 1], -width)[0:1], (TILE, lanes))
+
+    @pl.when(core == 1)
+    def _():
+        for l in range(depth):
+            T4[l, tiles + 1] = jnp.broadcast_to(T4[l, tiles, TILE - 1 : TILE], (TILE, lanes))
+            EP[l, blocks + 1] = jnp.broadcast_to(lane_rows(EP[l, blocks], width)[TILE - 1 : TILE], (TILE, lanes))
+
+    def stage(l, s, c):
+        own = EP[l, 1 + s]
+        if c == 0:
+            M[l, s, c, 0] = pltpu.roll(jnp.where(group == GROUPS - 1, EP[l, s], own), lax.rem(spin + width, lanes), 1)
+            M[l, s, c, 1:3] = T4[l, GROUPS * s : GROUPS * s + 2]
+        else:
+            M[l, s, c, 1:3] = T4[l, GROUPS * s + 4 : GROUPS * s + 6]
+            M[l, s, c, 3] = pltpu.roll(jnp.where(group == 0, EP[l, s + 2], own), lax.rem(spin + lanes - width, lanes), 1)
+
+    late = ((0, 0), (blocks - 1, 1))
+    for l in range(depth):
+        for s in range(blocks):
+            for c in range(2):
+                M[l, s, c, 3 - 3 * c] = T4[l, GROUPS * s + 2 + c]
+                if (s, c) not in late:
+                    stage(l, s, c)
+
+    table.wait()
     senders = jnp.where(here, 2 * (n_az // n_rad - 1) + 1, 2 * (n_az // n_rad) + 1)
     pl.semaphore_wait(barrier, senders)
 
@@ -832,7 +1303,7 @@
     return pl.pallas_call(
         functools.partial(turned_kernel, n_az, n_rad),
         out_shape=pltpu.VMEM(state.shape, state.dtype),
-        in_specs=[pl.BlockSpec(memory_space=pl.ANY), pl.BlockSpec(memory_space=pltpu.VMEM)],
+        in_specs=[pl.BlockSpec(memory_space=pl.ANY)] * 2,
         out_specs=pl.BlockSpec(memory_space=pltpu.VMEM),
         scratch_shapes=[
             vmem(fields, depth, width, lanes),
@@ -841,6 +1312,7 @@
             vmem(depth, blocks, 2, 4, *tile),
             vmem(n_az, 5, *tile),
             pltpu.VMEM((1, lanes), jnp.int32),
+            pltpu.VMEM((1, lanes), jnp.int32),
             pltpu.VMEM((2 * lanes + 2 * TILE, lanes), jnp.int32),
             pltpu.VMEM((4 * TILE, lanes), jnp.int32),
             vmem(GROUPS * fields, 4 * TILE, lanes),
@@ -848,6 +1320,7 @@
             vmem(n_az, 2 * TILE + TILE // 2, lanes),
             vmem(depth, blocks, 2, 2 * TILE + TILE // 2, lanes),
             dma((depth,)),
+            dma(()),
             dma((2,)),
             dma((4, depth)),
             dma((2, n_az)),

time: 22.9 us -> 22.2 us (0.969)
  Pallas kernels: 22 us -> 21.4 us
    pallas_call x1, Pallas kernels: 22 us -> 21.4 us  [turned_body(): pl.pallas_call(functools.partial(turned_kernel, n_az, n_rad), out_shape=p...]
where the time goes in v8:
time: 22.2 us; the launch traced here: 22.1 us
  Pallas kernels  21.4 us (96%)
  local copies, waits for them, and re-layouts  0.67 us (3%)
    pallas_call x1, Pallas kernels, turned_body(): pl.pallas_call(functools.partial(turned_kernel, n_az, n_rad), out_shape=p...  21.4 us
    unnamed x1, local copies, waits for them, and re-layouts  0.67 us

profile of v8, /device:TPU:0, one launch (start us, length us, event | category | flops | bytes accessed | tf_op | source)
XLA Modules:
  0.0 22.1 jit_solution(4367137433086038926)
XLA Ops:
  0.0 21.4 %shard_map.28 = f32[5,2,32,128]{3,2,1,0:T(8,128)S(1)} custom-call(f32[5,2,32,128]{3,2,1,0:T(8,128)} %x_in.1, s32[1,128]{1,0:T(1,128)} %bitcast.1), custom_call_target="tpu_custom_call" | custom-call | tf_op jit(solution)/shard_map/pallas_call | solution.py:1303
  21.4 0.7 %copy.4 = f32[5,2,32,128]{3,2,1,0:T(8,128)} copy(f32[5,2,32,128]{3,2,1,0:T(8,128)S(1)} %shard_map.28) | data formatting | bytes 327680

commit v9 on v6

--- a/solution.py
+++ b/solution.py
@@ -364,7 +364,7 @@
 
 
 def tiles_of(x):
-    return [x[g * TILE : (g + 1) * TILE] for g in range(GROUPS)]
+    return [x[g : g + TILE] for g in range(0, x.shape[0], TILE)]
 
 
 def next_of(x, axis):
@@ -399,28 +399,26 @@
     return flux - last_of(flux, axis)
 
 
-def line_push(pressure, density, speed, axis, courant):
+def line_push(pressure, density, speed, axis):
     compress = jnp.minimum(next_of(speed, axis) - last_of(speed, axis), 0.0)
-    total = pressure + VISCOSITY_COEF * density * compress * compress
+    total = pressure + density * compress * compress
     work = total * speed
-    scale = -0.5 * courant
-    return scale * (next_of(total, axis) - last_of(total, axis)), scale * (next_of(work, axis) - last_of(work, axis))
+    return next_of(total, axis) - last_of(total, axis), next_of(work, axis) - last_of(work, axis)
 
 
 def advect_all(state):
     rho, mr, mp = state[:3]
-    az_speeds, rad_speeds = [], []
+    span = len(rho[0])
     inverse = [tiles_of(1.0 / across(rho, u)) for u in range(GROUPS)]
-    for g in range(GROUPS):
-        az_speeds.append(line_speeds(along(mp, g) * along(inverse, g), 1, COURANT_AZIMUTH))
-        rad_speeds.append(line_speeds(across(mr, g) * across(inverse, g), 0, COURANT_RADIAL))
+    az_speeds = [line_speeds(along(mp, w) * along(inverse, w), 1, COURANT_AZIMUTH) for w in range(span)]
+    rad_speeds = [line_speeds(across(mr, u) * across(inverse, u), 0, COURANT_RADIAL) for u in range(GROUPS)]
 
     def step(field):
-        turned = [along(field, w) for w in range(GROUPS)]
-        turned = [tiles_of(turned[w] - line_advect(turned[w], az_speeds[w], 1)) for w in range(GROUPS)]
+        turned = [along(field, w) for w in range(span)]
+        turned = [tiles_of(turned[w] - line_advect(turned[w], az_speeds[w], 1)) for w in range(span)]
         out = []
         for u in range(GROUPS):
-            rest = line([turned[w][u] for w in range(GROUPS)])
+            rest = line([turned[w][u] for w in range(span)])
             out.append(tiles_of(rest - line_advect(across(field, u), rad_speeds[u], 0)))
         return out
 
@@ -428,64 +426,87 @@
 
 
 def push_all(state):
+    scale = -0.5 * COURANT_AZIMUTH
+    assert COURANT_RADIAL == COURANT_AZIMUTH
     rho, mr, mp, mz, energy = state
-    inverse, pressure, new_mr, rest = [], [], [], []
+    inverse, pressure, density, new_mr, rest = [], [], [], [], []
     for u in range(GROUPS):
         r, a, b, c, e = (across(f, u) for f in state)
         inv = 1.0 / r
-        p = (GAMMA_GAS - 1.0) * (e - 0.5 * (a * a + b * b + c * c) * inv)
-        rad_m, rad_e = line_push(p, r, a * inv, 0, COURANT_RADIAL)
+        p = (scale * (GAMMA_GAS - 1.0)) * (e - 0.5 * (a * a + b * b + c * c) * inv)
+        d = (scale * VISCOSITY_COEF) * r
+        rad_m, rad_e = line_push(p, d, a * inv, 0)
         inverse.append(tiles_of(inv))
         pressure.append(tiles_of(p))
+        density.append(tiles_of(d))
         new_mr.append(tiles_of(a + rad_m))
         rest.append(tiles_of(e + rad_e))
-    new_mp = [[None] * GROUPS for _ in range(GROUPS)]
-    new_energy = [[None] * GROUPS for _ in range(GROUPS)]
-    for w in range(GROUPS):
+    span = len(rho[0])
+    new_mp = [[None] * span for _ in range(GROUPS)]
+    new_energy = [[None] * span for _ in range(GROUPS)]
+    for w in range(span):
         b = along(mp, w)
-        az_m, az_e = line_push(along(pressure, w), along(rho, w), b * along(inverse, w), 1, COURANT_AZIMUTH)
+        az_m, az_e = line_push(along(pressure, w), along(density, w), b * along(inverse, w), 1)
         for u, (m, e) in enumerate(zip(tiles_of(b + az_m), tiles_of(along(rest, w) + az_e))):
             new_mp[u][w], new_energy[u][w] = m, e
     return new_mr, new_mp, new_energy
 
 
-def turned_kernel(n_az, n_rad, x_in, shifts, out, *scratch):
-    (x, T4, EP, M, W, other, SC, AM, F, G, B, R, load_sem, shift_sem, swap_sem, out_send, out_recv, pass_send, pass_recv,
-     back_send, back_recv) = scratch
+def turned_kernel(n_az, n_rad, x_in, shifts_in, out, *scratch):
+    (x, T4, EP, M, W, shifts, other, SC, AM, F, G, B, R, load_sem, table_sem, shift_sem, swap_sem, out_send, out_recv,
+     pass_send, pass_recv, back_send, back_recv) = scratch
     fields, depth, width, lanes = x.shape
-    blocks = n_az // (depth * n_rad)
+    plane = n_az // GROUPS
+    workers = n_az // 2
+    blocks = workers // (depth * n_rad)
     tiles = lanes // TILE
-    rows = 4 * TILE
+    quads = tiles // GROUPS
+    own = tiles // (2 * blocks)
+    span = own + 2
+    parts = span + 1
+    rows = span * TILE
     MESH = pl.DeviceIdType.MESH
     me = lax.axis_index("az")
     core = lax.axis_index("rad")
-    half = lax.rem(me, n_rad)
-    layer = lax.rem(me // n_rad, depth)
-    block = me // (n_rad * depth)
+    half = lax.rem(me // depth, n_rad)
+    layer = lax.rem(me, depth)
+    block = me // plane - 1
+    works = jnp.logical_and(block >= 0, block < blocks)
     place = (half * blocks + block) * 2 + core
     partner = {"rad": 1 - core}
     here = half == core
+    stays = jnp.logical_and(works, here)
 
     def remote(src, dst, send, recv, where):
         return pltpu.make_async_remote_copy(
             src_ref=src, dst_ref=dst, send_sem=send, recv_sem=recv, device_id=where, device_id_type=MESH
         )
 
+    def arrived(dst, recv):
+        return pltpu.make_async_copy(dst, dst, recv)
+
+    barrier = pltpu.get_barrier_semaphore()
+
+    @pl.when(works)
+    def _():
+        for k in range(n_az - 1):
+            pl.semaphore_signal(
+                barrier, inc=1, device_id={"az": k + (me <= k).astype(jnp.int32), "rad": half}, device_id_type=MESH
+            )
+
+    pl.semaphore_signal(barrier, inc=1, device_id=partner, device_id_type=MESH)
     loads = [pltpu.make_async_copy(x_in.at[:, l], x.at[:, l], load_sem.at[l]) for l in range(depth)]
     for load in loads:
         load.start()
-    barrier = pltpu.get_barrier_semaphore()
-    for k in range(1, n_az):
-        pl.semaphore_signal(
-            barrier, inc=1, device_id={"az": lax.rem(me + k, n_az), "rad": half}, device_id_type=MESH
-        )
-    pl.semaphore_signal(barrier, inc=1, device_id=partner, device_id_type=MESH)
+    table = pltpu.make_async_copy(shifts_in, shifts, table_sem)
+    table.start()
 
     lane = lax.broadcasted_iota(jnp.int32, (TILE, lanes), 1)
     row = lax.broadcasted_iota(jnp.int32, (TILE, lanes), 0)
+    lane_of = {n * TILE: lax.broadcasted_iota(jnp.int32, (n * TILE, lanes), 1) for n in (1, 2, own)}
     group = lane // width
-
     spin = me * TILE
+    unspin = lax.rem(lanes - spin, lanes)
 
     def rows_of(f, l):
         return [x[f, l, pl.ds(u, width // GROUPS, stride=GROUPS), :] for u in range(GROUPS)]
@@ -497,7 +518,7 @@
     energy = [part for l in range(depth) for part in rows_of(4, l)]
     turned = jnp.concatenate(energy * (lanes // (depth * width)), axis=0).T.reshape(tiles, TILE, lanes)
     for l in range(depth):
-        for m in range(tiles // GROUPS):
+        for m in range(quads):
             packed = turned[GROUPS * m] if l == 0 else lane_rows(turned[GROUPS * m], -width * l)
             for g in range(1, GROUPS):
                 packed = jnp.where(group == g, lane_rows(turned[GROUPS * m + g], width * (g - l)), packed)
@@ -513,65 +534,46 @@
     def _():
         for l in range(depth):
             T4[l, tiles + 1] = jnp.broadcast_to(T4[l, tiles, TILE - 1 : TILE], (TILE, lanes))
-            EP[l, blocks + 1] = jnp.broadcast_to(lane_rows(EP[l, blocks], width)[TILE - 1 : TILE], (TILE, lanes))
+            EP[l, quads + 1] = jnp.broadcast_to(lane_rows(EP[l, quads], width)[TILE - 1 : TILE], (TILE, lanes))
+
+    def energy_of(l, m):
+        joined = jnp.where(group == GROUPS - 1, EP[l, m], EP[l, m + 1])
+        return pltpu.roll(joined, lax.rem(spin + width, lanes), 1)
 
     def stage(l, s, c):
-        own = EP[l, 1 + s]
+        first = 2 * own * s + c * (own + 1)
         if c == 0:
-            M[l, s, c, 0] = pltpu.roll(jnp.where(group == GROUPS - 1, EP[l, s], own), lax.rem(spin + width, lanes), 1)
-            M[l, s, c, 1:3] = T4[l, GROUPS * s : GROUPS * s + 2]
+            M[l, s, c, 0], M[l, s, c, 1] = energy_of(l, 2 * s), energy_of(l, 2 * s + 1)
+            M[l, s, c, 2 : own + 2] = T4[l, first : first + own]
         else:
-            M[l, s, c, 1:3] = T4[l, GROUPS * s + 4 : GROUPS * s + 6]
-            M[l, s, c, 3] = pltpu.roll(jnp.where(group == 0, EP[l, s + 2], own), lax.rem(spin + lanes - width, lanes), 1)
+            M[l, s, c, 1 : own + 1] = T4[l, first + 1 : first + own + 1]
+            M[l, s, c, own + 1], M[l, s, c, own + 2] = energy_of(l, 2 * s + 1), energy_of(l, 2 * s + 2)
 
     late = ((0, 0), (blocks - 1, 1))
     for l in range(depth):
         for s in range(blocks):
             for c in range(2):
-                M[l, s, c, 3 - 3 * c] = T4[l, GROUPS * s + 2 + c]
+                M[l, s, c, (parts - 1) * (1 - c)] = T4[l, 2 * own * s + own + c]
                 if (s, c) not in late:
                     stage(l, s, c)
 
-    senders = jnp.where(here, 2 * (n_az // n_rad - 1) + 1, 2 * (n_az // n_rad) + 1)
-    pl.semaphore_wait(barrier, senders)
-
-    swap_shift = remote(shifts, other, shift_sem.at[0], shift_sem.at[1], partner)
-    swap_shift.start()
-
-    def swaps(l, up):
-        src = (tiles, blocks) if up else (1, 1)
-        dst = (0, 0) if up else (tiles + 1, blocks + 1)
-        return [
-            remote(T4.at[l, src[0]], T4.at[l, dst[0]], swap_sem.at[0, l], swap_sem.at[1, l], partner),
-            remote(EP.at[l, src[1]], EP.at[l, dst[1]], swap_sem.at[2, l], swap_sem.at[3, l], partner),
-        ]
-
-    @pl.when(core == 0)
-    def _():
-        for l in range(depth):
-            for copy in swaps(l, True):
-                copy.start()
-
-    @pl.when(core == 1)
-    def _():
-        for l in range(depth):
-            for copy in swaps(l, False):
-                copy.start()
-
-    targets = [(ks, kl, kc) for ks in (2, 1, 3, 0) for kl in range(depth) for kc in (1, 0)]
+    table.wait()
+    pl.semaphore_wait(barrier, jnp.where(stays, 2 * (workers // n_rad) - 1, 2 * (workers // n_rad) + 1))
+
+    targets = [(ks, kl, kc) for ks in (1, 0) for kl in (1, 0) for kc in (0, 1)]
 
     def send(index, first):
         ks, kl, kc = targets[index]
-        s = lax.rem(block + ks, blocks)
+        s = lax.rem(me // plane + 1 + ks, blocks)
         l = lax.rem(layer + kl, depth)
         c = lax.rem(core + kc, 2)
         if first:
-            src, dst = M.at[l, s, c, 3 - 3 * c], W.at[me, 3 - 2 * c]
+            src, dst = M.at[l, s, c, (parts - 1) * (1 - c)], W.at[me, (parts - 1) - (parts - 2) * c]
             sems = out_send.at[0, index], out_recv.at[0, me]
         else:
-            src, dst = M.at[l, s, c, pl.ds(c, 3)], W.at[me, pl.ds(2 * c, 3)]
+            src, dst = M.at[l, s, c, pl.ds(c, parts - 1)], W.at[me, pl.ds(2 * c, parts - 1)]
             sems = out_send.at[1, index], out_recv.at[1, me]
-        sent = remote(src, dst, *sems, {"az": (s * depth + l) * n_rad + core, "rad": c})
+        sent = remote(src, dst, *sems, {"az": (1 + s) * plane + core * depth + l, "rad": c})
         is_late = s == c * (blocks - 1)
         return sent, None if ks or kl or kc else pltpu.make_async_copy(src, dst, sems[1]), is_late
 
@@ -582,13 +584,37 @@
                 sent.start()
                 continue
             now = True if when is None else when(is_late)
-            for copy, also in ((sent, None),) if within is None else ((within, here), (sent, jnp.logical_not(here))):
+            for copy, also in ((sent, None),) if within is None else ((within, stays), (sent, jnp.logical_not(stays))):
 
                 @pl.when(now if also is None else jnp.logical_and(now, also))
                 def _():
                     copy.start()
 
     start(True)
+
+    swap_shift = remote(shifts, other, shift_sem.at[0], shift_sem.at[1], partner)
+    swap_shift.start()
+
+    def swaps(l, up):
+        src = (tiles, quads) if up else (1, 1)
+        dst = (0, 0) if up else (tiles + 1, quads + 1)
+        return [
+            remote(T4.at[l, src[0]], T4.at[l, dst[0]], swap_sem.at[0, l], swap_sem.at[1, l], partner),
+            remote(EP.at[l, src[1]], EP.at[l, dst[1]], swap_sem.at[2, l], swap_sem.at[3, l], partner),
+        ]
+
+    @pl.when(core == 0)
+    def _():
+        for l in range(depth):
+            for copy in swaps(l, True):
+                copy.start()
+
+    @pl.when(core == 1)
+    def _():
+        for l in range(depth):
+            for copy in swaps(l, False):
+                copy.start()
+
     start(False, jnp.logical_not)
     for l in range(depth):
         for copy in swaps(l, True):
@@ -597,149 +623,152 @@
         for s, c in late:
             stage(l, s, c)
     start(False, lambda is_late: is_late)
-
     swap_shift.wait_recv()
-    lower = jnp.full((1, lanes), core, jnp.int32) == 0
-    mine, theirs = shifts[...], other[...]
-    for c in range(2):
-        part = jnp.where(lower, mine if c == 0 else theirs, theirs if c == 0 else mine)
-        table = jnp.broadcast_to(part.astype(jnp.float32), (lanes, lanes)).T.astype(jnp.int32)
-        SC[TILE + c * lanes : TILE + (c + 1) * lanes] = table
-    SC[0:TILE] = jnp.zeros((TILE, lanes), jnp.int32)
-    SC[TILE + 2 * lanes :] = jnp.zeros((TILE, lanes), jnp.int32)
-    AM[...] = SC[pl.ds(pl.multiple_of(place * 2 * TILE, TILE), rows)]
-    amounts = [AM[pl.ds(w, TILE, stride=GROUPS), :] for w in range(GROUPS)]
-    coarse = [amount // GROUPS for amount in amounts]
-    odd = [(amount & 1) != 0 for amount in amounts]
-    two = [(amount & 2) != 0 for amount in amounts]
-    source = [
-        [(lane - coarse[w] - jnp.where(u < (amounts[w] & (GROUPS - 1)), 1, 0)) & (lanes - 1) for w in range(GROUPS)]
-        for u in range(GROUPS)
-    ]
-
-    plane = n_az // GROUPS
-    near = [lax.rem(me // plane + k, GROUPS) for k in (0, 1, 3, 2)]
 
     def passes(k):
-        ahead = pl.ds(near[k] * plane, plane)
-        return remote(W.at[ahead, 3 - 2 * core], W.at[ahead, 4 * core], pass_send.at[k], pass_recv.at[near[k]], partner)
+        q = lax.rem(me // plane + k, GROUPS)
+        ahead = pl.ds(q * plane, plane)
+        src, dst = W.at[ahead, (parts - 1) - (parts - 2) * core], W.at[ahead, parts * core]
+        return remote(src, dst, pass_send.at[k], pass_recv.at[q], partner)
 
     def passed(q):
-        return remote(
-            W.at[pl.ds(q * plane, plane), 3 - 2 * core], W.at[pl.ds(q * plane, plane), 4 - 4 * core],
-            pass_send.at[q], pass_recv.at[q], partner
-        )
-
-    def arrived(dst, recv):
-        return pltpu.make_async_copy(dst, dst, recv)
-
-    for k in range(GROUPS):
-        for j in range(plane):
-            i = near[k] * plane + lax.rem(me + j, plane)
-            arrived(W.at[i, 3 - 2 * core], out_recv.at[0, i]).wait()
-        passes(k).start()
-
-    def rotate(field):
-        out = [[None] * GROUPS for _ in range(GROUPS)]
-        for w in range(GROUPS):
-            near_by = [jnp.where(odd[w], field[u - 1][w], field[u][w]) for u in range(GROUPS)]
-            for u in range(GROUPS):
-                chosen = jnp.where(two[w], near_by[u - 2], near_by[u])
-                out[u][w] = jnp.take_along_axis(chosen, source[u][w], axis=1)
-        return out
-
-    at = jnp.full((TILE, lanes), place, jnp.int32)
-    lowest = jnp.logical_and(at == 0, row < 2)
-    highest = jnp.logical_and(at == 2 * blocks * n_rad - 1, row >= TILE - 2)
-
-    def edged(field):
-        out = []
-        for u in range(GROUPS):
-            low = jnp.broadcast_to(field[u][0][2:3], (TILE, lanes))
-            high = jnp.broadcast_to(field[u][3][TILE - 3 : TILE - 2], (TILE, lanes))
-            out.append(
-                [jnp.where(highest, high, field[u][w]) for w in range(2)]
-                + [jnp.where(lowest, low, field[u][w]) for w in range(2, GROUPS)]
-            )
-        return out
-
-    def unpack(parts):
-        return [lane_rows(part, -TILE * g) for g, part in enumerate(exchange(parts, lane_of[parts[0].shape[0]]))]
-
-    lane_of = {n * TILE: lax.broadcasted_iota(jnp.int32, (n * TILE, lanes), 1) for n in (1, 2, 3)}
-
-    for k in range(GROUPS):
-        for j in range(plane):
-            i = near[k] * plane + lax.rem(me + j, plane)
-            arrived(W.at[i, pl.ds(2 * core, 3)], out_recv.at[1, i]).wait()
-    direct = unpack([W[i, 1:4].reshape(3 * TILE, lanes) for i in range(n_az)])
-    for g in range(GROUPS * GROUPS):
-        F[g, pl.ds(pl.multiple_of(core * TILE, TILE), 3 * TILE)] = direct[g]
-    for g, part in enumerate(unpack([W[i, 4 * core] for i in range(n_az)])):
-        w, u = g // GROUPS, g % GROUPS
-        F[GROUPS * GROUPS + u, w * TILE : (w + 1) * TILE] = part
-    for q in range(GROUPS):
-        passed(q).wait_recv()
-    for g, part in enumerate(unpack([W[i, 4 - 4 * core] for i in range(n_az)])):
-        F[g, pl.ds(pl.multiple_of((1 - core) * 3 * TILE, TILE), TILE)] = part
-
-    state = [
-        [[F[GROUPS * f + u, pl.ds(w, TILE, stride=GROUPS), :] for w in range(GROUPS)] for u in range(GROUPS)]
-        for f in range(fields)
-    ]
-    step = advect_all(state)
-    state = [edged(rotate(step(field))) for field in state]
-    mr, mp, en = push_all(state)
-    state = [edged(field) for field in (state[0], mr, mp, state[3], en)]
-    step = advect_all(state)
-    state = [edged(rotate(step(field))) for field in state]
-    mr, mp, en = push_all(state)
-    for f, field in enumerate((state[0], mr, mp, state[3], en)):
-        for u in range(GROUPS):
-            for w in range(GROUPS):
-                G[GROUPS * f + u, pl.ds(w, TILE, stride=GROUPS), :] = field[u][w]
-
-    order = [(k, j) for k in (2, 1, 3, 0) for j in [*range(1, plane), 0]]
-
-    def back(index):
-        k, j = order[index]
-        n = order.index((k, j))
+        return arrived(W.at[pl.ds(q * plane, plane), parts * (1 - core)], pass_recv.at[q])
+
+    order = range(n_az)
+
+    def back(n):
         if n == 0:
             i = 0
-        elif n < 4:
-            i = 1 + lax.rem(me + n - 1, 3)
-        elif n < 8:
-            i = 4 + lax.rem(me + n + 1, 4)
+        elif n < plane:
+            i = 1 + lax.rem(me + n - 1, plane - 1)
+        elif n < 2 * plane:
+            i = plane + lax.rem(me + n + 1, plane)
         else:
-            i = 8 + lax.rem(me + n + 1, 8)
+            i = 2 * plane + lax.rem(me + n + 1, 2 * plane)
         src, dst = B.at[i], R.at[layer, block, core]
-        sems = back_send.at[index], back_recv.at[(layer * blocks + block) * 2 + core]
+        sems = back_send.at[n], back_recv.at[(layer * blocks + block) * 2 + core]
         sent = remote(src, dst, *sems, {"az": i, "rad": half})
-        return sent, None if n not in (0, 3, 7, 15) else pltpu.make_async_copy(src, dst, sems[1]), i == me
-
-    own = [lane_rows(G[g, TILE : 3 * TILE], TILE * g) for g in range(GROUPS * GROUPS)]
-    for i, part in enumerate(exchange(own, lane_of[2 * TILE])):
-        B[i, : 2 * TILE] = part
-    own = [
-        lane_rows(G[GROUPS * GROUPS + u, (1 + t) * TILE : (2 + t) * TILE], TILE * (GROUPS * t + u))
-        for t in range(2)
-        for u in range(GROUPS)
-    ]
-    for i, part in enumerate(exchange(own, lane)):
-        folded = fold(lane_rows(part, -TILE * i), lane, row)
-        B[i, 2 * TILE :] = folded[: TILE // 2]
-        B[i + n_az // 2, 2 * TILE :] = folded[TILE // 2 :]
-    for index in range(len(order)):
-        sent, within, same = back(index)
-        if within is None:
-            sent.start()
-        else:
-
-            @pl.when(jnp.logical_and(here, same))
+        return sent, pltpu.make_async_copy(src, dst, sems[1]) if n in (2 * plane - 1, n_az - 1) else None, me == i
+
+    @pl.when(works)
+    def _():
+        lower = jnp.full((1, lanes), core, jnp.int32) == 0
+        mine, theirs = shifts[...], other[...]
+        for c in range(2):
+            part = jnp.where(lower, mine if c == 0 else theirs, theirs if c == 0 else mine)
+            along_lanes = jnp.broadcast_to(part.astype(jnp.float32), (lanes, lanes)).T.astype(jnp.int32)
+            SC[TILE + c * lanes : TILE + (c + 1) * lanes] = along_lanes
+        SC[0:TILE] = jnp.zeros((TILE, lanes), jnp.int32)
+        SC[TILE + 2 * lanes :] = jnp.zeros((TILE, lanes), jnp.int32)
+        AM[...] = SC[pl.ds(pl.multiple_of(place * own * TILE, TILE), rows)]
+        amounts = [AM[pl.ds(w, TILE, stride=span), :] for w in range(span)]
+        coarse = [amount // GROUPS for amount in amounts]
+        odd = [(amount & 1) != 0 for amount in amounts]
+        two = [(amount & 2) != 0 for amount in amounts]
+        source = [
+            [
+                (lane - coarse[w] - jnp.where(u < (amounts[w] & (GROUPS - 1)), 1, 0)) & (lanes - 1)
+                for w in range(span)
+            ]
+            for u in range(GROUPS)
+        ]
+
+        for k in (0, 1, 3, 2):
+            for j in range(plane):
+                i = lax.rem(me // plane + k, GROUPS) * plane + lax.rem(me + j, plane)
+                arrived(W.at[i, (parts - 1) - (parts - 2) * core], out_recv.at[0, i]).wait()
+            passes(k).start()
+
+        def rotate(field):
+            done = [[None] * span for _ in range(GROUPS)]
+            for w in range(span):
+                near_by = [jnp.where(odd[w], field[u - 1][w], field[u][w]) for u in range(GROUPS)]
+                for u in range(GROUPS):
+                    chosen = jnp.where(two[w], near_by[u - 2], near_by[u])
+                    done[u][w] = jnp.take_along_axis(chosen, source[u][w], axis=1)
+            return done
+
+        at = jnp.full((TILE, lanes), place, jnp.int32)
+        is_low = at == 0
+        is_high = at == 2 * blocks * n_rad - 1
+        end_low, end_high = TILE, TILE * (1 + own) - 1
+
+        def replaced(field, at_row, by_row, where):
+            w, sub = by_row % span, by_row // span
+            mask = jnp.logical_and(where, row == at_row // span)
+            for u in range(GROUPS):
+                end = jnp.broadcast_to(field[u][w][sub : sub + 1], (TILE, lanes))
+                field[u][at_row % span] = jnp.where(mask, end, field[u][at_row % span])
+
+        def edged(field):
+            field = [list(tiles_u) for tiles_u in field]
+            for k in (1, 2):
+                replaced(field, end_low - k, end_low, is_low)
+                replaced(field, end_high + k, end_high, is_high)
+            return field
+
+        def unpack(pieces):
+            return [lane_rows(p, -TILE * g) for g, p in enumerate(exchange(pieces, lane_of[pieces[0].shape[0]]))]
+
+        def settle(slot, count, at_row):
+            pieces = [W[i, pl.ds(slot, count)].reshape(count * TILE, lanes) for i in range(n_az)]
+            for g, piece in enumerate(unpack(pieces)):
+                F[g, pl.ds(pl.multiple_of(at_row, TILE), count * TILE)] = piece
+
+        for q in range(GROUPS):
+            passed(q).wait()
+        settle((parts - 1) * (1 - core), 2, own * TILE * (1 - core))
+        for k in (0, 1, 3, 2):
+            for j in range(plane):
+                i = lax.rem(me // plane + k, GROUPS) * plane + lax.rem(me + j, plane)
+                arrived(W.at[i, pl.ds(2 * core, parts - 1)], out_recv.at[1, i]).wait()
+        settle(2, own, 2 * TILE * core)
+        pieces = [W[i, pl.ds((parts - 1) * core, 2)].reshape(2 * TILE, lanes) for i in range(n_az)]
+        for g, piece in enumerate(unpack(pieces)):
+            for t in range(2):
+                w, u = GROUPS * t + g // GROUPS, g % GROUPS
+                if w < span:
+                    F[GROUPS * GROUPS + u, w * TILE : (w + 1) * TILE] = piece[t * TILE : (t + 1) * TILE]
+
+        state = [
+            [[F[GROUPS * f + u, pl.ds(w, TILE, stride=span), :] for w in range(span)] for u in range(GROUPS)]
+            for f in range(fields)
+        ]
+        step = advect_all(state)
+        state = [edged(rotate(step(field))) for field in state]
+        mr, mp, en = push_all(state)
+        state = [edged(field) for field in (state[0], mr, mp, state[3], en)]
+        step = advect_all(state)
+        state = [edged(rotate(step(field))) for field in state]
+        mr, mp, en = push_all(state)
+        for f, field in enumerate((state[0], mr, mp, state[3], en)):
+            for u in range(GROUPS):
+                for w in range(span):
+                    G[GROUPS * f + u, pl.ds(w, TILE, stride=span), :] = field[u][w]
+
+        mine = slice(TILE, (1 + own) * TILE)
+        kept = [lane_rows(G[g, mine], TILE * g) for g in range(GROUPS * GROUPS)]
+        for i, piece in enumerate(exchange(kept, lane_of[own * TILE])):
+            B[i, : own * TILE] = piece
+        kept = [
+            lane_rows(G[GROUPS * GROUPS + u, (1 + t) * TILE : (2 + t) * TILE], TILE * (GROUPS * t + u))
+            for t in range(own)
+            for u in range(GROUPS)
+        ]
+        for i, piece in enumerate(exchange(kept, lane)):
+            B[i, own * TILE :] = piece
+
+        for n in order:
+            sent, within, mine = back(n)
+            if within is None:
+                sent.start()
+                continue
+
+            @pl.when(jnp.logical_and(here, mine))
             def _():
                 within.start()
 
-            @pl.when(jnp.logical_not(jnp.logical_and(here, same)))
+            @pl.when(jnp.logical_not(jnp.logical_and(here, mine)))
             def _():
                 sent.start()
 
@@ -747,21 +776,21 @@
         for s in range(blocks):
             for c in range(2):
                 arrived(R.at[l, s, c], back_recv.at[(l * blocks + s) * 2 + c]).wait()
-    for l in range(depth):
-        pieces = [R[l, s, c, : 2 * TILE] for s in range(blocks) for c in range(2)]
-        cells = pltpu.roll(jnp.concatenate(pieces, axis=0), lax.rem(lanes - spin, lanes), 1).T
+        pieces = [R[l, s, c, : own * TILE] for s in range(blocks) for c in range(2)]
+        cells = pltpu.roll(jnp.concatenate(pieces, axis=0), unspin, 1).T
         for f in range(GROUPS):
             for u in range(GROUPS):
                 g = GROUPS * f + u
                 out[f, l, pl.ds(u, TILE, stride=GROUPS), :] = cells[g * TILE : (g + 1) * TILE]
     pieces = []
     for s in range(blocks):
-        both = [fold(jnp.concatenate([R[l, s, c, 2 * TILE :] for c in range(2)], axis=0), lane, row) for l in range(depth)]
-        for g in range(GROUPS):
-            piece = lane_rows(both[0], -width * g)
-            for l in range(1, depth):
-                piece = jnp.where(group == l, lane_rows(both[l], width * (l - g)), piece)
-            pieces.append(piece)
+        for c in range(2):
+            both = [pltpu.roll(R[l, s, c, own * TILE :], unspin, 1) for l in range(depth)]
+            for g in range(GROUPS):
+                piece = lane_rows(both[0], -width * g)
+                for l in range(1, depth):
+                    piece = jnp.where(group == l, lane_rows(both[l], width * (l - g)), piece)
+                pieces.append(piece)
     cells = jnp.concatenate(pieces, axis=0).T
     for l in range(depth):
         for u in range(GROUPS):
@@ -779,19 +808,21 @@
                 sent.wait_send()
             else:
 
-                @pl.when(jnp.logical_not(here))
+                @pl.when(jnp.logical_not(stays))
                 def _():
                     sent.wait_send()
 
-    for k in range(GROUPS):
-        passes(k).wait_send()
-    for index in range(len(order)):
-        sent, within, same = back(index)
-        if within is None:
-            sent.wait_send()
-        else:
-
-            @pl.when(jnp.logical_not(jnp.logical_and(here, same)))
+    @pl.when(works)
+    def _():
+        for k in range(GROUPS):
+            passes(k).wait_send()
+        for n in order:
+            sent, within, mine = back(n)
+            if within is None:
+                sent.wait_send()
+                continue
+
+            @pl.when(jnp.logical_not(jnp.logical_and(here, mine)))
             def _():
                 sent.wait_send()
 
@@ -799,30 +830,33 @@
 def turned_body(mesh, state, shifts):
     n_az, n_rad = mesh.shape["az"], mesh.shape["rad"]
     fields, depth, width, lanes = state.shape
-    blocks = n_az // (depth * n_rad)
+    blocks = n_az // 2 // (depth * n_rad)
     tiles = lanes // TILE
+    own = tiles // (2 * blocks)
     vmem = lambda *shape: pltpu.VMEM(shape, jnp.float32)
     dma = pltpu.SemaphoreType.DMA
     tile = (TILE, lanes)
     return pl.pallas_call(
         functools.partial(turned_kernel, n_az, n_rad),
         out_shape=pltpu.VMEM(state.shape, state.dtype),
-        in_specs=[pl.BlockSpec(memory_space=pl.ANY), pl.BlockSpec(memory_space=pltpu.VMEM)],
+        in_specs=[pl.BlockSpec(memory_space=pl.ANY)] * 2,
         out_specs=pl.BlockSpec(memory_space=pltpu.VMEM),
         scratch_shapes=[
             vmem(fields, depth, width, lanes),
             vmem(depth, tiles + 2, *tile),
-            vmem(depth, blocks + 2, *tile),
-            vmem(depth, blocks, 2, 4, *tile),
-            vmem(n_az, 5, *tile),
+            vmem(depth, tiles // GROUPS + 2, *tile),
+            vmem(depth, blocks, 2, own + 3, *tile),
+            vmem(n_az, own + 4, *tile),
+            pltpu.VMEM((1, lanes), jnp.int32),
             pltpu.VMEM((1, lanes), jnp.int32),
             pltpu.VMEM((2 * lanes + 2 * TILE, lanes), jnp.int32),
-            pltpu.VMEM((4 * TILE, lanes), jnp.int32),
-            vmem(GROUPS * fields, 4 * TILE, lanes),
-            vmem(GROUPS * fields, 4 * TILE, lanes),
-            vmem(n_az, 2 * TILE + TILE // 2, lanes),
-            vmem(depth, blocks, 2, 2 * TILE + TILE // 2, lanes),
+            pltpu.VMEM(((own + 2) * TILE, lanes), jnp.int32),
+            vmem(GROUPS * fields, (own + 2) * TILE, lanes),
+            vmem(GROUPS * fields, (own + 2) * TILE, lanes),
+            vmem(n_az, (own + 1) * TILE, lanes),
+            vmem(depth, blocks, 2, (own + 1) * TILE, lanes),
             dma((depth,)),
+            dma(()),
             dma((2,)),
             dma((4, depth)),
             dma((2, n_az)),
@@ -842,14 +876,12 @@
     tiles = lanes // TILE
     return (
         n_rad == 2
+        and depth == 2
         and fields == GROUPS + 1
-        and width * GROUPS == lanes
-        and n_az == GROUPS * GROUPS
         and width == GROUPS * TILE
         and lanes == n_az * TILE
-        and n_az % (depth * n_rad) == 0
-        and tiles == GROUPS * (n_az // (depth * n_rad))
-        and depth * width <= lanes
+        and n_az == GROUPS * GROUPS
+        and tiles == n_az
         and SMAX <= lanes
     )
 

time: 23.2 us -> 22.3 us (0.961)
  Pallas kernels: 22.3 us -> 21.4 us
    pallas_call x1, Pallas kernels: 22.3 us -> 21.4 us  [turned_body(): pl.pallas_call(functools.partial(turned_kernel, n_az, n_rad), out_shape=p...]
where the time goes in v9:
time: 22.3 us; the launch traced here: 22.1 us
  Pallas kernels  21.4 us (96%)
  local copies, waits for them, and re-layouts  0.67 us (3%)
    pallas_call x1, Pallas kernels, turned_body(): pl.pallas_call(functools.partial(turned_kernel, n_az, n_rad), out_shape=p...  21.4 us
    unnamed x1, local copies, waits for them, and re-layouts  0.67 us

profile of v9, /device:TPU:0, one launch (start us, length us, event | category | flops | bytes accessed | tf_op | source)
XLA Modules:
  0.0 22.1 jit_solution(12571414703672186345)
XLA Ops:
  0.0 21.4 %shard_map.28 = f32[5,2,32,128]{3,2,1,0:T(8,128)S(1)} custom-call(f32[5,2,32,128]{3,2,1,0:T(8,128)} %x_in.1, s32[1,128]{1,0:T(1,128)} %bitcast.1), custom_call_target="tpu_custom_call" | custom-call | tf_op jit(solution)/shard_map/pallas_call | solution.py:839
  21.4 0.7 %copy.4 = f32[5,2,32,128]{3,2,1,0:T(8,128)} copy(f32[5,2,32,128]{3,2,1,0:T(8,128)S(1)} %shard_map.28) | data formatting | bytes 327680

commit v10 on v9

--- a/solution.py
+++ b/solution.py
@@ -453,7 +453,7 @@
 
 
 def turned_kernel(n_az, n_rad, x_in, shifts_in, out, *scratch):
-    (x, T4, EP, M, W, shifts, other, SC, AM, F, G, B, R, load_sem, table_sem, shift_sem, swap_sem, out_send, out_recv,
+    (x, T4, EP, M, W, shifts, other, SC, AM, F, FE, K, G, B, R, load_sem, table_sem, shift_sem, swap_sem, out_send, out_recv,
      pass_send, pass_recv, back_send, back_recv) = scratch
     fields, depth, width, lanes = x.shape
     plane = n_az // GROUPS
@@ -560,7 +560,7 @@
     table.wait()
     pl.semaphore_wait(barrier, jnp.where(stays, 2 * (workers // n_rad) - 1, 2 * (workers // n_rad) + 1))
 
-    targets = [(ks, kl, kc) for ks in (1, 0) for kl in (1, 0) for kc in (0, 1)]
+    targets = [(ks, kl, kc) for ks in (0, 1) for kl in (1, 0) for kc in (0, 1)]
 
     def send(index, first):
         ks, kl, kc = targets[index]
@@ -661,51 +661,57 @@
         SC[0:TILE] = jnp.zeros((TILE, lanes), jnp.int32)
         SC[TILE + 2 * lanes :] = jnp.zeros((TILE, lanes), jnp.int32)
         AM[...] = SC[pl.ds(pl.multiple_of(place * own * TILE, TILE), rows)]
-        amounts = [AM[pl.ds(w, TILE, stride=span), :] for w in range(span)]
-        coarse = [amount // GROUPS for amount in amounts]
-        odd = [(amount & 1) != 0 for amount in amounts]
-        two = [(amount & 2) != 0 for amount in amounts]
-        source = [
-            [
-                (lane - coarse[w] - jnp.where(u < (amounts[w] & (GROUPS - 1)), 1, 0)) & (lanes - 1)
-                for w in range(span)
+        at = jnp.full((TILE, lanes), place, jnp.int32)
+        is_low = at == 0
+        is_high = at == 2 * blocks * n_rad - 1
+
+        def tools_of(span, start):
+            amounts = [AM[pl.ds(start + w, TILE, stride=span), :] for w in range(span)]
+            odd = [(amount & 1) != 0 for amount in amounts]
+            two = [(amount & 2) != 0 for amount in amounts]
+            source = [
+                [
+                    (lane - amounts[w] // GROUPS - jnp.where(u < (amounts[w] & (GROUPS - 1)), 1, 0)) & (lanes - 1)
+                    for w in range(span)
+                ]
+                for u in range(GROUPS)
             ]
-            for u in range(GROUPS)
-        ]
+
+            def rotate(field):
+                done = [[None] * span for _ in range(GROUPS)]
+                for w in range(span):
+                    near_by = [jnp.where(odd[w], field[u - 1][w], field[u][w]) for u in range(GROUPS)]
+                    for u in range(GROUPS):
+                        chosen = jnp.where(two[w], near_by[u - 2], near_by[u])
+                        done[u][w] = jnp.take_along_axis(chosen, source[u][w], axis=1)
+                return done
+
+            end_low, end_high = TILE - start, TILE * (1 + own) - 1 - start
+
+            def replaced(field, at_row, by_row, where):
+                w, sub = by_row % span, by_row // span
+                mask = jnp.logical_and(where, row == at_row // span)
+                for u in range(GROUPS):
+                    end = jnp.broadcast_to(field[u][w][sub : sub + 1], (TILE, lanes))
+                    field[u][at_row % span] = jnp.where(mask, end, field[u][at_row % span])
+
+            def edged(field):
+                field = [list(tiles_u) for tiles_u in field]
+                for k in (1, 2):
+                    replaced(field, end_low - k, end_low, is_low)
+                    replaced(field, end_high + k, end_high, is_high)
+                return field
+
+            return rotate, edged
+
+        rotate, edged = tools_of(span, 0)
+        rotate_core, edged_core = tools_of(span - 1, GROUPS)
 
         for k in (0, 1, 3, 2):
             for j in range(plane):
                 i = lax.rem(me // plane + k, GROUPS) * plane + lax.rem(me + j, plane)
                 arrived(W.at[i, (parts - 1) - (parts - 2) * core], out_recv.at[0, i]).wait()
             passes(k).start()
-
-        def rotate(field):
-            done = [[None] * span for _ in range(GROUPS)]
-            for w in range(span):
-                near_by = [jnp.where(odd[w], field[u - 1][w], field[u][w]) for u in range(GROUPS)]
-                for u in range(GROUPS):
-                    chosen = jnp.where(two[w], near_by[u - 2], near_by[u])
-                    done[u][w] = jnp.take_along_axis(chosen, source[u][w], axis=1)
-            return done
-
-        at = jnp.full((TILE, lanes), place, jnp.int32)
-        is_low = at == 0
-        is_high = at == 2 * blocks * n_rad - 1
-        end_low, end_high = TILE, TILE * (1 + own) - 1
-
-        def replaced(field, at_row, by_row, where):
-            w, sub = by_row % span, by_row // span
-            mask = jnp.logical_and(where, row == at_row // span)
-            for u in range(GROUPS):
-                end = jnp.broadcast_to(field[u][w][sub : sub + 1], (TILE, lanes))
-                field[u][at_row % span] = jnp.where(mask, end, field[u][at_row % span])
-
-        def edged(field):
-            field = [list(tiles_u) for tiles_u in field]
-            for k in (1, 2):
-                replaced(field, end_low - k, end_low, is_low)
-                replaced(field, end_high + k, end_high, is_high)
-            return field
 
         def unpack(pieces):
             return [lane_rows(p, -TILE * g) for g, p in enumerate(exchange(pieces, lane_of[pieces[0].shape[0]]))]
@@ -728,23 +734,40 @@
             for t in range(2):
                 w, u = GROUPS * t + g // GROUPS, g % GROUPS
                 if w < span:
-                    F[GROUPS * GROUPS + u, w * TILE : (w + 1) * TILE] = piece[t * TILE : (t + 1) * TILE]
+                    FE[u, w * TILE : (w + 1) * TILE] = piece[t * TILE : (t + 1) * TILE]
+
+        def source_of(f, u):
+            return FE.at[u] if f == GROUPS else F.at[GROUPS * f + u]
 
         state = [
-            [[F[GROUPS * f + u, pl.ds(w, TILE, stride=span), :] for w in range(span)] for u in range(GROUPS)]
+            [[source_of(f, u)[pl.ds(w, TILE, stride=span), :] for w in range(span)] for u in range(GROUPS)]
             for f in range(fields)
         ]
-        step = advect_all(state)
-        state = [edged(rotate(step(field))) for field in state]
-        mr, mp, en = push_all(state)
-        state = [edged(field) for field in (state[0], mr, mp, state[3], en)]
         step = advect_all(state)
         state = [edged(rotate(step(field))) for field in state]
         mr, mp, en = push_all(state)
         for f, field in enumerate((state[0], mr, mp, state[3], en)):
             for u in range(GROUPS):
                 for w in range(span):
-                    G[GROUPS * f + u, pl.ds(w, TILE, stride=span), :] = field[u][w]
+                    K[GROUPS * f + u, pl.ds(w, TILE, stride=span), :] = field[u][w]
+
+        inner = range(span - 1)
+        state = [
+            edged_core(
+                [
+                    [K[GROUPS * f + u, pl.ds(GROUPS + w, TILE, stride=span - 1), :] for w in inner]
+                    for u in range(GROUPS)
+                ]
+            )
+            for f in range(fields)
+        ]
+        step = advect_all(state)
+        state = [edged_core(rotate_core(step(field))) for field in state]
+        mr, mp, en = push_all(state)
+        for f, field in enumerate((state[0], mr, mp, state[3], en)):
+            for u in range(GROUPS):
+                for w in inner:
+                    G[GROUPS * f + u, pl.ds(GROUPS + w, TILE, stride=span - 1), :] = field[u][w]
 
         mine = slice(TILE, (1 + own) * TILE)
         kept = [lane_rows(G[g, mine], TILE * g) for g in range(GROUPS * GROUPS)]
@@ -851,6 +874,8 @@
             pltpu.VMEM((1, lanes), jnp.int32),
             pltpu.VMEM((2 * lanes + 2 * TILE, lanes), jnp.int32),
             pltpu.VMEM(((own + 2) * TILE, lanes), jnp.int32),
+            vmem(GROUPS * GROUPS, (own + 2) * TILE, lanes),
+            vmem(GROUPS, (own + 2) * TILE, lanes),
             vmem(GROUPS * fields, (own + 2) * TILE, lanes),
             vmem(GROUPS * fields, (own + 2) * TILE, lanes),
             vmem(n_az, (own + 1) * TILE, lanes),

time: 22.3 us -> 21.5 us (0.964)
  Pallas kernels: 21.4 us -> 20.6 us
    pallas_call x1, Pallas kernels: 21.4 us -> 20.6 us  [turned_body(): pl.pallas_call(functools.partial(turned_kernel, n_az, n_rad), out_shape=p...]
where the time goes in v10:
time: 21.5 us; the launch traced here: 21.3 us
  Pallas kernels  20.6 us (96%)
  local copies, waits for them, and re-layouts  0.67 us (3%)
    pallas_call x1, Pallas kernels, turned_body(): pl.pallas_call(functools.partial(turned_kernel, n_az, n_rad), out_shape=p...  20.6 us
    unnamed x1, local copies, waits for them, and re-layouts  0.67 us

profile of v10, /device:TPU:0, one launch (start us, length us, event | category | flops | bytes accessed | tf_op | source)
XLA Modules:
  0.0 21.3 jit_solution(10907758258708362282)
XLA Ops:
  0.0 20.6 %shard_map.28 = f32[5,2,32,128]{3,2,1,0:T(8,128)S(1)} custom-call(f32[5,2,32,128]{3,2,1,0:T(8,128)} %x_in.1, s32[1,128]{1,0:T(1,128)} %bitcast.1), custom_call_target="tpu_custom_call" | custom-call | tf_op jit(solution)/shard_map/pallas_call | solution.py:862
  20.6 0.7 %copy.4 = f32[5,2,32,128]{3,2,1,0:T(8,128)} copy(f32[5,2,32,128]{3,2,1,0:T(8,128)S(1)} %shard_map.28) | data formatting | bytes 327680

commit v11 on v10

--- a/solution.py
+++ b/solution.py
@@ -387,7 +387,7 @@
 
 def line_speeds(velocity, axis, courant):
     face = (0.5 * courant) * (velocity + next_of(velocity, axis))
-    return jnp.maximum(face, 0.0), jnp.minimum(face, 0.0)
+    return face, face > 0
 
 
 def line_advect(field, speeds, axis):
@@ -395,7 +395,7 @@
     high = next_of(low, axis)
     product = low * high
     half = jnp.where(product > 0, product / (low + high), 0.0)
-    flux = speeds[0] * (field + half) + speeds[1] * next_of(field - half, axis)
+    flux = speeds[0] * jnp.where(speeds[1], field + half, next_of(field - half, axis))
     return flux - last_of(flux, axis)
 
 
@@ -560,7 +560,7 @@
     table.wait()
     pl.semaphore_wait(barrier, jnp.where(stays, 2 * (workers // n_rad) - 1, 2 * (workers // n_rad) + 1))
 
-    targets = [(ks, kl, kc) for ks in (0, 1) for kl in (1, 0) for kc in (0, 1)]
+    targets = [(ks, kl, kc) for ks in (0, 1) for kc in (1, 0) for kl in (1, 0)]
 
     def send(index, first):
         ks, kl, kc = targets[index]

time: 21.5 us -> 21.4 us (level)
  no operation moved by 1% of the time
where the time goes in v11:
time: 21.4 us; the launch traced here: 21.3 us
  Pallas kernels  20.6 us (96%)
  local copies, waits for them, and re-layouts  0.67 us (3%)
    pallas_call x1, Pallas kernels, turned_body(): pl.pallas_call(functools.partial(turned_kernel, n_az, n_rad), out_shape=p...  20.6 us
    unnamed x1, local copies, waits for them, and re-layouts  0.67 us

profile of v11, /device:TPU:0, one launch (start us, length us, event | category | flops | bytes accessed | tf_op | source)
XLA Modules:
  0.0 21.3 jit_solution(11222711195713605488)
XLA Ops:
  0.0 20.6 %shard_map.28 = f32[5,2,32,128]{3,2,1,0:T(8,128)S(1)} custom-call(f32[5,2,32,128]{3,2,1,0:T(8,128)} %x_in.1, s32[1,128]{1,0:T(1,128)} %bitcast.1), custom_call_target="tpu_custom_call" | custom-call | tf_op jit(solution)/shard_map/pallas_call | solution.py:862
  20.6 0.7 %copy.4 = f32[5,2,32,128]{3,2,1,0:T(8,128)} copy(f32[5,2,32,128]{3,2,1,0:T(8,128)S(1)} %shard_map.28) | data formatting | bytes 327680
